TPU v7x, 32 devices: a whole 2x2x4 slice. The times are simulated.
32 devices in a mesh: ctx: 16 (over z, y, core), fsdp: 2 (over x).
Axes of the slice: x: 2, y: 2, z: 4, core: 2. Of those that a mesh axis runs over, the one named last changes fastest.
Arguments:
- queries: bfloat16 [2, 2048, 2048], P('fsdp', 'ctx'), may hold values from -8 to 8
- keys_values: bfloat16 [2, 2048, 2, 2048], P('fsdp', 'ctx'), may hold values from -8 to 8
- upstream: bfloat16 [2, 2048, 2048], P('fsdp', 'ctx'), may hold values from -6 to 6
- out_weight: bfloat16 [2048, 2048], P('fsdp'), may hold values from -0.125 to 0.125
Outputs:
- grad_queries: bfloat16 [2, 2048, 2048], P('fsdp', 'ctx')
- grad_keys_values: bfloat16 [2, 2048, 2, 2048], P('fsdp', 'ctx')
- grad_weight: float32 [2048, 2048], P(('ctx', 'fsdp'))
All inputs are finite; a program needn't handle non-finite values.
Results may differ from a plain program's by a relative error of at most 0.014.
Values may be sent and summed in bfloat16 or wider, within the bound.
A program may use at most 128 MiB of HBM per device.

v0:
```python
import functools

import jax
import jax.numpy as jnp
from jax import lax
from jax.experimental import pallas as pl
from jax.experimental.pallas import tpu as pltpu
from jax.sharding import PartitionSpec as P

HEADS = 16
HEAD_DIM = 128
SPAN = 4
WINDOW = 512
NEGATIVE = -1e30
CHUNKS = 8
AHEAD = 5
LAG = 2
DELAY = 4
F32 = jnp.float32
BF16 = jnp.bfloat16


class Place:
    def __init__(self, planes, fsdp):
        self.planes, self.fsdp = planes, fsdp
        me = lax.axis_index("ctx")
        self.f = lax.axis_index("fsdp")
        self.p = lax.div(me, SPAN)
        self.r = lax.rem(me, SPAN)
        self.core = lax.rem(self.r, 2)
        self.y = lax.div(self.r, 2)
        self.mate = self.r + 1 - 2 * self.core
        self.across = lax.rem(self.r + 2, SPAN)

    def dev(self, p, r, f):
        return {"ctx": p * SPAN + r, "fsdp": f}

    def members(self):
        for dr in range(SPAN):
            for df in range(self.fsdp):
                if dr or df:
                    yield lax.rem(self.r + dr, SPAN), lax.rem(self.f + df, self.fsdp), dr, df

    def barrier(self):
        sem = pltpu.get_barrier_semaphore()
        count = 0
        for r, f, _, _ in self.members():
            pl.semaphore_signal(sem, inc=1, device_id=self.dev(self.p, r, f), device_id_type=pl.DeviceIdType.MESH)
            count += 1
        for dp in range(1, self.planes):
            other = lax.rem(self.p + dp, self.planes)
            pl.semaphore_signal(sem, inc=1, device_id=self.dev(other, self.r, self.f), device_id_type=pl.DeviceIdType.MESH)
            count += 1
        pl.semaphore_wait(sem, count)


def remote(src, dst, send, recv, device):
    return pltpu.make_async_remote_copy(
        src_ref=src, dst_ref=dst, send_sem=send, recv_sem=recv, device_id=device, device_id_type=pl.DeviceIdType.MESH
    )


def chunk_cols(c, wide):
    return pl.ds(pl.multiple_of(c * wide, wide), wide)


def attend_head(q, ga, k, v, bias):
    inv_root = HEAD_DIM ** (-0.5)
    nt = (((1,), (1,)), ((), ()))
    tn = (((0,), (0,)), ((), ()))
    scores = lax.dot_general(q, k, nt, preferred_element_type=F32) * inv_root + bias
    lifted = jnp.exp(scores - jnp.max(scores, axis=-1, keepdims=True))
    prob = lifted * (1.0 / jnp.sum(lifted, axis=-1, keepdims=True))
    low = prob.astype(BF16)
    att = jnp.dot(low, v, preferred_element_type=F32).astype(BF16)
    products = lax.dot_general(ga, v, nt, preferred_element_type=F32)
    center = jnp.sum(ga.astype(F32) * att.astype(F32), axis=-1, keepdims=True)
    ds = (prob * (products - center)).astype(BF16)
    dq = (jnp.dot(ds, k, preferred_element_type=F32) * inv_root).astype(BF16)
    dk = lax.dot_general(ds, q, tn, preferred_element_type=F32) * inv_root
    dv = lax.dot_general(low, ga, tn, preferred_element_type=F32)
    return att, dq, dk, dv


def layer_kernel(
    planes, fsdp,
    q_ref, kv, up, up_cols, weight,
    dq_ref, out_kv, out_w,
    w_v, up_in, part_out, part_in, win, ga_ref, up_all, bias,
    g, dkv, share_in, y_in, c_in, z_in, att_all, w_out, w_in,
    fz_send, fy_send, fc_send, fs_send, slot_recv, w_sem, u_send, u_recv, q_send, q_recv, m_send, m_recv,
    sh_send, sh_recv, y_send, y_recv, c_send, c_recv, z_send, z_recv,
    a_send, a_recv, b_send, b_recv, r_send, r_recv,
):
    at = Place(planes, fsdp)
    toks = up.shape[0]
    depth = weight.shape[0]
    width = weight.shape[1]
    wide = width // CHUNKS
    f = at.f
    mine = at.r * fsdp + f
    mate_across = lax.rem(at.mate + 2, SPAN)
    mate = at.dev(at.p, at.mate, f)
    over = at.dev(at.p, at.across, f)
    w_copy = pltpu.make_async_copy(weight, w_v, w_sem)
    w_copy.start()

    @pl.when(at.p == 0)
    def _():
        win[at.r] = jnp.zeros(win.shape[1:], BF16)

    at.barrier()

    def cut(ref, c):
        return ref.at[:, :, chunk_cols(c, wide)]

    def up_copy(df):
        h = lax.rem(f + df, fsdp)
        return remote(
            up.at[:, pl.ds(pl.multiple_of(h * depth, 128), depth)], up_in.at[fsdp - df], u_send.at[df], u_recv.at[fsdp - df],
            at.dev(at.p, at.r, h),
        )

    def slot(j, c):
        return cut(win.at[j], c)

    def fz_copy(c):
        return remote(cut(kv, c), slot(at.r, c), fz_send.at[c], slot_recv.at[at.r, c], at.dev(at.p + 1, at.r, f))

    def fy_copy(c, src):
        return remote(src, slot(at.r, c), fy_send.at[c], slot_recv.at[at.r, c], over)

    def fc_copy(c, src):
        return remote(src, slot(at.r, c), fc_send.at[c], slot_recv.at[at.r, c], mate)

    def fs_copy(c):
        return remote(slot(at.across, c), slot(at.across, c), fs_send.at[c], slot_recv.at[at.across, c], mate)

    def arrived(j, c):
        remote(slot(j, c), slot(j, c), fz_send.at[c], slot_recv.at[j, c], mate).wait_recv()

    for df in range(1, fsdp):
        up_copy(df).start()

    def begin(c, _):
        @pl.when(at.p < planes - 1)
        def _():
            fz_copy(c).start()

        @pl.when(at.y == 0)
        def _():
            fy_copy(c, cut(kv, c)).start()

        @pl.when(at.core == 0)
        def _():
            fc_copy(c, cut(kv, c)).start()

        return 0

    lax.fori_loop(0, CHUNKS, begin, 0)

    row = lax.broadcasted_iota(jnp.int32, (toks, toks), 0)
    col = lax.broadcasted_iota(jnp.int32, (toks, toks), 1)
    for j in range(SPAN + 1):
        if j < SPAN:
            blocks = jnp.where(j < at.r, at.r - j, at.r - j + SPAN)
            limit = jnp.where(jnp.logical_and(at.p == 0, j >= at.r), 0, WINDOW)
        else:
            blocks, limit = 0, WINDOW
        distance = blocks * toks + row - col
        bias[:, j * toks : (j + 1) * toks] = jnp.where((distance >= 0) & (distance < limit), 0.0, NEGATIVE)

    w_copy.wait()
    tile = 512

    def product(lhs_of, put):
        def step(t, _):
            cols = chunk_cols(t, tile)
            put(cols, jnp.dot(lhs_of(), w_v[:, cols], preferred_element_type=F32))
            return 0

        lax.fori_loop(0, width // tile, step, 0)

    def part_copy(df):
        return remote(
            part_out.at[df], part_in.at[fsdp - df], q_send.at[df], q_recv.at[fsdp - df],
            at.dev(at.p, at.r, lax.rem(f + df, fsdp)),
        )

    for df in range(1, fsdp):
        remote(up_in.at[df], up_in.at[df], u_send.at[df], u_recv.at[df], at.dev(at.p, at.r, lax.rem(f + df, fsdp))).wait_recv()

        def put(cols, value, df=df):
            part_out[df, :, cols] = value.astype(BF16)

        product(lambda df=df: up_in[df], put)
        part_copy(df).start()

    def col_copy(r, h, dr, df):
        return remote(up_cols.at[r * fsdp + h], up_all.at[mine], m_send.at[dr, df], m_recv.at[dr, df], at.dev(at.p, r, h))

    for r, h, dr, df in at.members():
        col_copy(r, h, dr, df).start()
    up_all[mine] = up_cols[mine]

    def forward(c, _):
        @pl.when(at.p > 0)
        def _():
            arrived(at.r, c)

        @pl.when(at.y == 1)
        def _():
            fy_copy(c, slot(at.r, c)).start()

        @pl.when(at.core == 1)
        def _():
            fc_copy(c, slot(at.r, c)).start()

        arrived(at.across, c)
        fs_copy(c).start()
        return 0

    lax.fori_loop(0, AHEAD, forward, 0)
    own_depth = pl.ds(pl.multiple_of(f * depth, 128), depth)
    for df in range(1, fsdp):
        remote(part_in.at[df], part_in.at[df], q_send.at[df], q_recv.at[df], at.dev(at.p, at.r, lax.rem(f + df, fsdp))).wait_recv()

    def put_own(cols, value):
        for df in range(1, fsdp):
            value = value + part_in[df, :, cols].astype(F32)
        ga_ref[:, cols] = value.astype(BF16)

    product(lambda: up[:, own_depth], put_own)

    def peers():
        for half in range(2):
            for df in range(fsdp):
                yield half, df, lax.rem(at.r + 2 * half, SPAN), lax.rem(f + df, fsdp)

    def a_copy(half, df, r, h, view, c):
        return remote(view(att_all.at[mine]), view(att_all.at[mine]), a_send.at[half, df], a_recv.at[half, df, c], at.dev(at.p, r, h))

    def origin(half, df):
        return lax.rem(at.r + SPAN - 2 * half, SPAN) * fsdp + lax.rem(f + fsdp - df, fsdp)

    def b_copy(half, df, view, c):
        block = att_all.at[origin(half, df)]
        return remote(view(block), view(block), b_send.at[half, df], b_recv.at[half, df, c], mate)

    def whole(ref):
        return ref

    def sh_copy(c):
        return remote(cut(g.at[mate_across], c), cut(share_in, c), sh_send.at[c], sh_recv.at[c], mate)

    def c_copy(c):
        return remote(cut(g.at[at.mate], c), cut(c_in, c), c_send.at[c], c_recv.at[c], mate)

    def y_copy(c):
        return remote(cut(g.at[at.across], c), cut(y_in, c), y_send.at[c], y_recv.at[c], over)

    def z_copy(c):
        return remote(cut(g.at[at.r], c), cut(z_in, c), z_send.at[c], z_recv.at[c], at.dev(at.p - 1, at.r, f))

    def second(c, _):
        cols = chunk_cols(c, wide)
        sh_copy(c).wait_recv()
        g[at.across, :, :, cols] = (g[at.across, :, :, cols].astype(F32) + share_in[:, :, cols].astype(F32)).astype(BF16)
        y_copy(c).start()
        return 0

    def third(c, _):
        cols = chunk_cols(c, wide)
        c_copy(c).wait_recv()
        y_copy(c).wait_recv()
        core_prev = at.core == 1
        y_prev = at.y == 1
        c_val = c_in[:, :, cols].astype(F32)
        y_val = y_in[:, :, cols].astype(F32)
        zero = jnp.zeros_like(c_val)
        prev = g[at.r, :, :, cols].astype(F32) + jnp.where(core_prev, c_val, zero) + jnp.where(y_prev, y_val, zero)
        g[at.r, :, :, cols] = prev.astype(BF16)
        dkv[:, :, cols] = dkv[:, :, cols] + jnp.where(core_prev, zero, c_val) + jnp.where(y_prev, zero, y_val)

        @pl.when(at.p > 0)
        def _():
            z_copy(c).start()

        return 0

    for r, h, dr, df in at.members():
        back = lax.rem(at.r + SPAN - dr, SPAN) * fsdp + lax.rem(f + fsdp - df, fsdp)
        remote(up_all.at[back], up_all.at[back], m_send.at[dr, df], m_recv.at[dr, df], at.dev(at.p, r, h)).wait_recv()
    own_rows = out_w.shape[0]
    tn = (((0,), (0,)), ((), ()))
    tokens = SPAN * fsdp * toks

    def r_copy(dp, view):
        other = lax.rem(at.p + dp, planes)
        return remote(
            view(w_out.at[other]), view(w_in.at[planes - dp]), r_send.at[dp], r_recv.at[planes - dp], at.dev(other, at.r, f)
        )

    def weigh(c, _):
        cols = chunk_cols(c, wide)

        def view(ref):
            return ref.at[:, cols]

        for half, df, r, h in peers():
            block = view(att_all.at[lax.rem(at.mate + SPAN - 2 * half, SPAN) * fsdp + lax.rem(f + fsdp - df, fsdp)])
            remote(block, block, b_send.at[half, df], b_recv.at[half, df, c], mate).wait_recv()
        lhs = up_all[...].reshape(tokens, up_all.shape[2])
        value = lax.dot_general(lhs, att_all[:, :, cols].reshape(tokens, wide), tn, preferred_element_type=F32)
        for n in range(planes):
            w_out[n, :, cols] = value[n * own_rows : (n + 1) * own_rows].astype(BF16)
        for dp in range(1, planes):
            r_copy(dp, view).start()
        return 0

    def relay(c, _):
        def view(ref):
            return ref.at[:, chunk_cols(c, wide)]

        for half, df, r, h in peers():
            if half or df:
                block = view(att_all.at[origin(half, df)])
                remote(block, block, a_send.at[half, df], a_recv.at[half, df, c], at.dev(at.p, r, h)).wait_recv()
                b_copy(half, df, view, c).start()

        @pl.when(c >= 1)
        def _():
            weigh(c - 1, 0)

        third(c, 0)
        return 0

    def attend(c, _):
        @pl.when(c + AHEAD < CHUNKS)
        def _():
            forward(c + AHEAD, 0)

        arrived(at.mate, c)
        arrived(mate_across, c)
        for h in range(wide // HEAD_DIM):
            cols = pl.ds(pl.multiple_of(c * wide + h * HEAD_DIM, HEAD_DIM), HEAD_DIM)
            k = jnp.concatenate([win[j, 0, :, cols] for j in range(SPAN)] + [kv[0, :, cols]], axis=0)
            v = jnp.concatenate([win[j, 1, :, cols] for j in range(SPAN)] + [kv[1, :, cols]], axis=0)
            att, dq, dk, dv = attend_head(q_ref[:, cols], ga_ref[:, cols], k, v, bias[...])
            att_all[mine, :, cols] = att
            dq_ref[:, cols] = dq
            for j in range(SPAN):
                g[j, 0, :, cols] = dk[j * toks : (j + 1) * toks].astype(BF16)
                g[j, 1, :, cols] = dv[j * toks : (j + 1) * toks].astype(BF16)
            dkv[0, :, cols] = dk[SPAN * toks :]
            dkv[1, :, cols] = dv[SPAN * toks :]

        def view(ref):
            return ref.at[:, chunk_cols(c, wide)]

        for half, df, r, h in peers():
            if half or df:
                a_copy(half, df, r, h, view, c).start()
        b_copy(0, 0, view, c).start()
        sh_copy(c).start()
        c_copy(c).start()

        @pl.when(c >= LAG)
        def _():
            second(c - LAG, 0)

        @pl.when(c >= DELAY)
        def _():
            relay(c - DELAY, 0)

        return 0

    lax.fori_loop(0, CHUNKS, attend, 0)
    lax.fori_loop(CHUNKS - LAG, CHUNKS, second, 0)

    lax.fori_loop(CHUNKS - DELAY, CHUNKS, relay, 0)
    weigh(CHUNKS - 1, 0)

    def fourth(c, _):
        cols = chunk_cols(c, wide)

        @pl.when(at.p < planes - 1)
        def _():
            z_copy(c).wait_recv()
            out_kv[:, :, cols] = (dkv[:, :, cols] + z_in[:, :, cols].astype(F32)).astype(BF16)

        @pl.when(at.p == planes - 1)
        def _():
            out_kv[:, :, cols] = dkv[:, :, cols].astype(BF16)

        @pl.when(at.p < planes - 1)
        def _():
            fz_copy(c).wait_send()

        fy_copy(c, slot(at.r, c)).wait_send()
        fc_copy(c, slot(at.r, c)).wait_send()
        fs_copy(c).wait_send()
        sh_copy(c).wait_send()
        c_copy(c).wait_send()
        y_copy(c).wait_send()

        @pl.when(at.p > 0)
        def _():
            z_copy(c).wait_send()

        return 0

    lax.fori_loop(0, CHUNKS, fourth, 0)
    for df in range(1, fsdp):
        up_copy(df).wait_send()
        part_copy(df).wait_send()
    for r, h, dr, df in at.members():
        col_copy(r, h, dr, df).wait_send()
    for half, df, r, h in peers():
        if half or df:
            a_copy(half, df, r, h, whole, 0).wait_send()
        b_copy(half, df, whole, 0).wait_send()
    out_w[...] = w_out[at.p].astype(F32)
    for dp in range(1, planes):
        remote(w_in.at[dp], w_in.at[dp], r_send.at[dp], r_recv.at[dp], at.dev(lax.rem(at.p + dp, planes), at.r, f)).wait_recv()
        out_w[...] += w_in[dp].astype(F32)
    for dp in range(1, planes):
        r_copy(dp, whole).wait_send()


def shards(queries, keys_values, upstream, out_weight):
    seqs, toks, width = queries.shape
    ctx, fsdp = lax.axis_size("ctx"), lax.axis_size("fsdp")
    planes = ctx // SPAN
    model = upstream.shape[2]
    own_rows = model // (ctx * fsdp)
    group = SPAN * fsdp
    cols = planes * own_rows
    depth = out_weight.shape[0]
    kv = jnp.swapaxes(keys_values[0], 0, 1)
    up = upstream[0]
    up_cols = up.reshape(toks, planes, SPAN, fsdp, own_rows).transpose(2, 3, 0, 1, 4).reshape(group, toks, cols)
    dma = pltpu.SemaphoreType.DMA
    any_spec = pl.BlockSpec(memory_space=pl.ANY)
    vm = pl.BlockSpec(memory_space=pltpu.VMEM)
    block = (2, toks, width)
    line = dma((CHUNKS,))
    fan = dma((2, fsdp))
    spread = dma((2, fsdp, CHUNKS))
    dq, out_kv, out_w = pl.pallas_call(
        functools.partial(layer_kernel, planes, fsdp),
        out_shape=(
            jax.ShapeDtypeStruct((toks, width), BF16),
            jax.ShapeDtypeStruct(block, BF16),
            jax.ShapeDtypeStruct((own_rows, width), F32),
        ),
        in_specs=[vm, vm, vm, vm, any_spec],
        out_specs=(vm, vm, vm),
        scratch_shapes=[
            pltpu.VMEM((depth, width), BF16),
            pltpu.VMEM((fsdp, toks, depth), BF16),
            pltpu.VMEM((fsdp, toks, width), BF16),
            pltpu.VMEM((fsdp, toks, width), BF16),
            pltpu.VMEM((SPAN,) + block, BF16),
            pltpu.VMEM((toks, width), BF16),
            pltpu.VMEM((group, toks, cols), BF16),
            pltpu.VMEM((toks, (SPAN + 1) * toks), F32),
            pltpu.VMEM((SPAN,) + block, BF16),
            pltpu.VMEM(block, F32),
            pltpu.VMEM(block, BF16),
            pltpu.VMEM(block, BF16),
            pltpu.VMEM(block, BF16),
            pltpu.VMEM(block, BF16),
            pltpu.VMEM((group, toks, width), BF16),
            pltpu.VMEM((planes, own_rows, width), BF16),
            pltpu.VMEM((planes, own_rows, width), BF16),
            line, line, line, line, dma((SPAN, CHUNKS)), dma,
            dma((fsdp,)), dma((fsdp,)), dma((fsdp,)), dma((fsdp,)), dma((SPAN, fsdp)), dma((SPAN, fsdp)),
            line, line, line, line, line, line, line, line,
            fan, spread, fan, spread, dma((planes,)), dma((planes,)),
        ],
        compiler_params=pltpu.CompilerParams(collective_id=0, has_side_effects=True),
        name="layer",
    )(queries[0], kv, up, up_cols, out_weight)
    return dq[None], jnp.swapaxes(out_kv, 0, 1)[None], out_w


def solution(mesh):
    return jax.shard_map(
        shards,
        mesh=mesh,
        in_specs=(
            P("fsdp", "ctx", None),
            P("fsdp", "ctx", None, None),
            P("fsdp", "ctx", None),
            P("fsdp", None),
        ),
        out_specs=(P("fsdp", "ctx", None), P("fsdp", "ctx", None, None), P(("ctx", "fsdp"), None)),
        check_vma=False,
    )
```

profile of v0, /device:TPU:4, one launch (start us, length us, event | category | flops | bytes accessed | tf_op | source)
XLA Modules:
  0.0 132.1 jit_solution(8360269706733750843)
XLA Ops:
  0.6 1.3 copy.11
  2.0 1.0 copy.13.up_cols
  3.0 2.5 %copy.16 = bf16[1,128,2,2048]{3,1,2,0:T(8,128)(2,1)} copy(bf16[1,128,2,2048]{3,2,1,0:T(2,128)(2,1)} %param.5) | data formatting | bytes 2097152 | tf_op args[1]
  5.5 119.5 %layer.1 = (bf16[128,2048]{1,0:T(8,128)(2,1)}, bf16[2,128,2048]{2,1,0:T(8,128)(2,1)}, f32[64,2048]{1,0:T(8,128)}) custom-call(bf16[128,2048]{1,0:T(8,128)(2,1)} %bitcast.21, bf16[2,128,2048]{2,1,0:T(8,128)(2,1)} %bitcast.15, bf16[128,2048]{1,0:T(8,128)(2,1)} %bitcast.18, bf16[8,128,256]{2,1,0:T(8,128)(2,1)} %copy.13.up_cols, bf16[1024,2048]{1,0:T(8,128)(2,1)} %weight.1), custom_call_target="tpu_custom_call" | custom-call | tf_op jit(solution)/shard_map/layer/pallas_call | solution.py:450
  125.1 3.3 %copy.14 = bf16[1,128,2,2048]{3,2,1,0:T(2,128)(2,1)} copy(bf16[1,128,2,2048]{3,1,2,0:T(8,128)(2,1)} %bitcast.19) | data formatting | bytes 2097152
  128.4 1.9 %copy.19 = bf16[1,128,2048]{2,1,0:T(8,128)(2,1)} copy(bf16[1,128,2048]{2,1,0:T(8,128)(2,1)} %bitcast.20) | data formatting | bytes 1048576
  130.2 1.9 %copy.20 = f32[64,2048]{1,0:T(8,128)} copy(f32[64,2048]{1,0:T(8,128)} %get-tuple-element.20) | data formatting | bytes 1048576
  (1 shorter events, 0.0 us)
where the time goes:
time: 132 us
  Pallas kernels  120 us (91%)
  local copies, waits for them, and re-layouts  11.9 us (9%)
    pallas_call x1, Pallas kernels, shards(): pl.pallas_call(functools.partial(layer_kernel, planes, fsdp), out_shape=(...  120 us
    unnamed x5, local copies, waits for them, and re-layouts  10.9 us

commit v1 on v0

v1 whole, which is shorter than its diff:
```python
import functools

import jax
import jax.numpy as jnp
from jax import lax
from jax.experimental import pallas as pl
from jax.experimental.pallas import tpu as pltpu
from jax.sharding import PartitionSpec as P

HEAD_DIM = 128
SPAN = 4
NEGATIVE = -1e30
F32 = jnp.float32
BF16 = jnp.bfloat16
NT = (((1,), (1,)), ((), ()))
TN = (((0,), (0,)), ((), ()))


def remote(src, dst, send, recv, device):
    return pltpu.make_async_remote_copy(
        src_ref=src, dst_ref=dst, send_sem=send, recv_sem=recv, device_id=device, device_id_type=pl.DeviceIdType.MESH
    )


def layer_kernel(
    planes, fsdp,
    q_in, kv_in, up_in, weight,
    dq_out, kv_out, out_w,
    q, kv, up, up_t, w, ga, att, low, bias, dq, dkv, dprev, dprev_in, dsum,
    gw_out, gw_in, zw_out, zw_in, fin_out, fin_in,
    own_sem, kv_s, kv_r, q_s, q_r, u_s, u_r, w_s, w_r, kz_s, kz_r,
    dq_s, dq_r, dz_s, dz_r, dk_s, dk_r, gx_s, gx_r, gz_s, gz_r, f_s, f_r,
):
    toks = q_in.shape[0]
    depth = weight.shape[0]
    width = weight.shape[1]
    quarter = width // SPAN
    heads = quarter // HEAD_DIM
    plane_toks = SPAN * toks
    keys = plane_toks + toks
    own_rows = out_w.shape[0]
    plane_rows = SPAN * own_rows
    inv_root = HEAD_DIM ** (-0.5)

    me = lax.axis_index("ctx")
    f = lax.axis_index("fsdp")
    p = lax.div(me, SPAN)
    r = lax.rem(me, SPAN)
    mate = r + 1 - 2 * lax.rem(r, 2)
    peer = [r, mate, lax.rem(r + 2, SPAN), lax.rem(mate + 2, SPAN)]
    not_first = p > 0
    not_last = p < planes - 1

    def dev(p_, r_, f_):
        return {"ctx": p_ * SPAN + r_, "fsdp": f_}

    def near(d):
        return dev(p, peer[d], f)

    def side(df):
        return lax.rem(f + df, fsdp)

    def level(dp):
        return lax.rem(p + dp, planes)

    def rows(i):
        return pl.ds(pl.multiple_of(i * toks, toks), toks)

    def own_plane(i):
        return pl.ds(pl.multiple_of(plane_toks + i * toks, toks), toks)

    def head(c):
        return pl.ds(c * HEAD_DIM, HEAD_DIM)

    def wide_head(i, c):
        return pl.ds(pl.multiple_of(i * quarter + c * HEAD_DIM, HEAD_DIM), HEAD_DIM)

    def quart(i):
        return pl.ds(pl.multiple_of(i * quarter, quarter), quarter)

    def w_rows(i):
        return pl.ds(pl.multiple_of(i * depth, depth), depth)

    own_copies = [
        pltpu.make_async_copy(kv_in.at[:, :, quart(r)], kv.at[:, own_plane(r), :], own_sem.at[0]),
        pltpu.make_async_copy(q_in.at[:, quart(r)], q.at[rows(r), :], own_sem.at[1]),
        pltpu.make_async_copy(up_in, up.at[rows(r), :], own_sem.at[2]),
        pltpu.make_async_copy(weight.at[:, quart(r)], w.at[w_rows(f), :], own_sem.at[3]),
    ]
    for copy in own_copies:
        copy.start()

    sem = pltpu.get_barrier_semaphore()
    targets = [near(d) for d in range(1, SPAN)]
    targets += [dev(p, r, side(df)) for df in range(1, fsdp)]
    targets += [dev(level(dp), r, f) for dp in range(1, planes)]
    for target in targets:
        pl.semaphore_signal(sem, inc=1, device_id=target, device_id_type=pl.DeviceIdType.MESH)
    pl.semaphore_wait(sem, len(targets))

    def kv_copy(d, c):
        return remote(kv_in.at[:, :, wide_head(peer[d], c)], kv.at[:, own_plane(r), head(c)], kv_s.at[d, c], kv_r.at[d, c], near(d))

    def kv_came(d, c):
        here = kv.at[:, own_plane(peer[d]), head(c)]
        remote(here, here, kv_s.at[d, c], kv_r.at[d, c], near(d)).wait_recv()

    def q_copy(d, c):
        return remote(q_in.at[:, wide_head(peer[d], c)], q.at[rows(r), head(c)], q_s.at[d, c], q_r.at[d, c], near(d))

    def q_came(d, c):
        here = q.at[rows(peer[d]), head(c)]
        remote(here, here, q_s.at[d, c], q_r.at[d, c], near(d)).wait_recv()

    def up_copy(d):
        if d == 3:
            here = up.at[rows(peer[2]), :]
            return remote(here, here, u_s.at[3], u_r.at[3], near(1))
        return remote(up_in, up.at[rows(r), :], u_s.at[d], u_r.at[d], near(d))

    def up_came(d):
        here = up.at[rows(peer[d]), :]
        remote(here, here, u_s.at[d], u_r.at[d], near(d)).wait_recv()

    def w_copy(df, c):
        return remote(
            weight.at[:, wide_head(r, c)], w.at[w_rows(f), head(c)], w_s.at[df, c], w_r.at[fsdp - df, c], dev(p, r, side(df))
        )

    def w_came(df, c):
        here = w.at[w_rows(side(df)), head(c)]
        remote(here, here, w_s.at[df, c], w_r.at[df, c], dev(p, r, side(df))).wait_recv()

    def kz_copy(d, c):
        src = kv_in.at[:, :, wide_head(r, c)] if d == 0 else kv.at[:, own_plane(peer[d]), head(c)]
        return remote(src, kv.at[:, rows(peer[d]), head(c)], kz_s.at[d, c], kz_r.at[d, c], dev(p + 1, r, f))

    def dq_copy(d, c):
        return remote(dq.at[rows(peer[d]), head(c)], dq_out.at[:, wide_head(r, c)], dq_s.at[d, c], dq_r.at[d, c], near(d))

    def dq_came(d, c):
        here = dq_out.at[:, wide_head(peer[d], c)]
        remote(here, here, dq_s.at[d, c], dq_r.at[d, c], near(d)).wait_recv()

    def own_dq(c):
        return pltpu.make_async_copy(dq.at[rows(r), head(c)], dq_out.at[:, wide_head(r, c)], dq_s.at[0, c])

    def dz_copy(c):
        return remote(dprev.at[:, :, head(c)], dprev_in.at[:, :, head(c)], dz_s.at[c], dz_r.at[c], dev(p - 1, r, f))

    def dk_copy(d, c):
        return remote(dsum.at[:, rows(peer[d]), head(c)], kv_out.at[:, :, wide_head(r, c)], dk_s.at[d, c], dk_r.at[d, c], near(d))

    def dk_came(d, c):
        here = kv_out.at[:, :, wide_head(peer[d], c)]
        remote(here, here, dk_s.at[d, c], dk_r.at[d, c], near(d)).wait_recv()

    def own_dk(c):
        return pltpu.make_async_copy(dsum.at[:, rows(r), head(c)], kv_out.at[:, :, wide_head(r, c)], dk_s.at[0, c])

    def gx_copy(df, c):
        return remote(
            gw_out.at[side(df), :, head(c)], gw_in.at[fsdp - df, :, head(c)], gx_s.at[df, c], gx_r.at[fsdp - df, c],
            dev(p, r, side(df)),
        )

    def gx_came(df, c):
        here = gw_in.at[df, :, head(c)]
        remote(here, here, gx_s.at[df, c], gx_r.at[df, c], dev(p, r, side(df))).wait_recv()

    def gz_copy(dp, c):
        return remote(
            zw_out.at[level(dp), :, head(c)], zw_in.at[planes - dp, :, head(c)], gz_s.at[dp, c], gz_r.at[planes - dp, c],
            dev(level(dp), r, f),
        )

    def gz_came(dp, c):
        here = zw_in.at[dp, :, head(c)]
        remote(here, here, gz_s.at[dp, c], gz_r.at[dp, c], dev(level(dp), r, f)).wait_recv()

    def f_copy(d, c):
        return remote(fin_out.at[peer[d], :, head(c)], fin_in.at[r, :, head(c)], f_s.at[d, c], f_r.at[d, c], near(d))

    def f_came(d, c):
        here = fin_in.at[peer[d], :, head(c)]
        remote(here, here, f_s.at[d, c], f_r.at[d, c], near(d)).wait_recv()

    around = range(1, SPAN)

    def spread(c):
        for d in around:
            kv_copy(d, c).start()
        for d in around:
            q_copy(d, c).start()

    for c in range(heads):
        @pl.when(not_last)
        def _(c=c):
            kz_copy(0, c).start()

        for df in range(1, fsdp):
            w_copy(df, c).start()
        spread(c)
        if c == 1:
            up_copy(2).start()
            up_copy(1).start()

    row = lax.broadcasted_iota(jnp.int32, (toks, keys), 0)
    col = lax.broadcasted_iota(jnp.int32, (toks, keys), 1)
    for b in range(SPAN):
        first = jnp.where(not_first, 0, plane_toks - b * toks)
        bias[b] = jnp.where((col > row) & (col <= row + plane_toks) & (col >= first), 0.0, NEGATIVE)
    dkv[...] = jnp.zeros(dkv.shape, F32)

    @pl.when(p == 0)
    def _():
        kv[:, :plane_toks] = jnp.zeros((2, plane_toks, quarter), BF16)

    def forward(c):
        for d in around:
            kv_came(d, c)

            @pl.when(not_last)
            def _(d=d):
                kz_copy(d, c).start()

    def window(b):
        return pl.ds(b * toks, keys)

    def attend(c):
        for d in around:
            q_came(d, c)

        @pl.when(not_first)
        def _():
            for d in range(SPAN):
                here = kv.at[:, rows(peer[d]), head(c)]
                remote(here, here, kz_s.at[d, c], kz_r.at[d, c], near(1)).wait_recv()

        for b in range(SPAN):
            block = pl.ds(b * toks, toks)
            scores = lax.dot_general(q[block, head(c)], kv[0, window(b), head(c)], NT, preferred_element_type=F32) * inv_root + bias[b]
            lifted = jnp.exp(scores - jnp.max(scores, axis=-1, keepdims=True))
            prob = (lifted * (1.0 / jnp.sum(lifted, axis=-1, keepdims=True))).astype(BF16)
            low[c * SPAN + b] = prob
            att[block, head(c)] = jnp.dot(prob, kv[1, window(b), head(c)], preferred_element_type=F32).astype(BF16)

    def backward(c):
        for b in range(SPAN):
            block = pl.ds(b * toks, toks)
            g = ga[block, head(c)]
            prob = low[c * SPAN + b]
            k = kv[0, window(b), head(c)]
            products = lax.dot_general(g, kv[1, window(b), head(c)], NT, preferred_element_type=F32)
            center = jnp.sum(g.astype(F32) * att[block, head(c)].astype(F32), axis=-1, keepdims=True)
            ds = (prob.astype(F32) * (products - center)).astype(BF16)
            dq[block, head(c)] = (jnp.dot(ds, k, preferred_element_type=F32) * inv_root).astype(BF16)
            dkv[0, window(b), head(c)] += lax.dot_general(ds, q[block, head(c)], TN, preferred_element_type=F32) * inv_root
            dkv[1, window(b), head(c)] += lax.dot_general(prob, g, TN, preferred_element_type=F32)
        for d in (2, 3, 1):
            dq_copy(d, c).start()
        own_dq(c).start()
        dprev[:, :, head(c)] = dkv[:, :plane_toks, head(c)].astype(BF16)

        @pl.when(not_first)
        def _():
            dz_copy(c).start()

    def collect(c):
        @pl.when(not_last)
        def _():
            dz_copy(c).wait_recv()
            dsum[:, :, head(c)] = (dkv[:, plane_toks:, head(c)] + dprev_in[:, :, head(c)].astype(F32)).astype(BF16)

        @pl.when(p == planes - 1)
        def _():
            dsum[:, :, head(c)] = dkv[:, plane_toks:, head(c)].astype(BF16)

        for d in (2, 3, 1):
            dk_copy(d, c).start()
        own_dk(c).start()

    pair = 2 * HEAD_DIM

    def project(g):
        for c in (2 * g, 2 * g + 1):
            for df in range(1, fsdp):
                w_came(df, c)
        for b in range(SPAN):
            block = pl.ds(b * toks, toks)
            ga[block, g * pair : (g + 1) * pair] = jnp.dot(
                up[block, :], w[:, g * pair : (g + 1) * pair], preferred_element_type=F32
            ).astype(BF16)

    tile = plane_toks
    unit = fsdp * own_rows

    def weigh(g):
        cols = slice(g * pair, (g + 1) * pair)

        def step(t, _):
            value = jnp.dot(up_t[pl.ds(pl.multiple_of(t * tile, tile), tile), :], att[:, cols], preferred_element_type=F32)
            value = value.reshape(tile // unit, fsdp, own_rows, pair)
            part = tile // fsdp
            for n in range(fsdp):
                gw_out[n, pl.ds(pl.multiple_of(t * part, part), part), cols] = value[:, n].reshape(part, pair).astype(BF16)
            return 0

        lax.fori_loop(0, up_t.shape[0] // tile, step, 0)
        for c in (2 * g, 2 * g + 1):
            for df in range(1, fsdp):
                gx_copy(df, c).start()

    def merge(c):
        total = gw_out[f, :, head(c)].astype(F32)
        for df in range(1, fsdp):
            gx_came(df, c)
            total = total + gw_in[df, :, head(c)].astype(F32)
        for n in range(planes):
            zw_out[n, :, head(c)] = total[n * plane_rows : (n + 1) * plane_rows].astype(BF16)
        for dp in range(1, planes):
            gz_copy(dp, c).start()

    def total_up(c):
        total = zw_out[p, :, head(c)].astype(F32)
        for dp in range(1, planes):
            gz_came(dp, c)
            total = total + zw_in[dp, :, head(c)].astype(F32)
        for n in range(SPAN):
            fin_out[n, :, head(c)] = total[n * own_rows : (n + 1) * own_rows].astype(BF16)
        for d in (2, 3, 1):
            f_copy(d, c).start()

    def finish(c):
        for d in around:
            f_came(d, c)
        out_w[:, wide_head(r, c)] = fin_out[r, :, head(c)].astype(F32)
        for d in around:
            out_w[:, wide_head(peer[d], c)] = fin_in[peer[d], :, head(c)].astype(F32)

    forward(0)
    forward(1)
    for copy in own_copies:
        copy.wait()
    attend(0)
    attend(1)
    up_came(2)
    up_copy(3).start()
    up_came(1)
    up_came(3)
    for i in range(up_t.shape[0] // tile):
        up_t[i * tile : (i + 1) * tile, :] = up[:, i * tile : (i + 1) * tile].T
    weigh(0)
    project(0)
    backward(0)
    forward(2)
    backward(1)
    merge(0)
    forward(3)
    attend(2)
    project(1)
    collect(0)
    merge(1)
    attend(3)
    weigh(1)
    total_up(0)
    backward(2)
    collect(1)
    total_up(1)
    backward(3)
    merge(2)
    collect(2)
    merge(3)
    total_up(2)
    collect(3)
    total_up(3)
    for c in range(heads):
        finish(c)

    for c in range(heads):
        for d in around:
            dq_came(d, c)
            dk_came(d, c)
            for copy in (kv_copy(d, c), q_copy(d, c), dq_copy(d, c), dk_copy(d, c), f_copy(d, c)):
                copy.wait_send()
        own_dq(c).wait()
        own_dk(c).wait()
        for df in range(1, fsdp):
            w_copy(df, c).wait_send()
            gx_copy(df, c).wait_send()
        for dp in range(1, planes):
            gz_copy(dp, c).wait_send()

        @pl.when(not_last)
        def _(c=c):
            for d in range(SPAN):
                kz_copy(d, c).wait_send()

        @pl.when(not_first)
        def _(c=c):
            dz_copy(c).wait_send()

    for d in around:
        up_copy(d).wait_send()


def shards(queries, keys_values, upstream, out_weight):
    seqs, toks, width = queries.shape
    ctx, fsdp = lax.axis_size("ctx"), lax.axis_size("fsdp")
    planes = ctx // SPAN
    model = upstream.shape[2]
    own_rows = model // (ctx * fsdp)
    quarter = width // SPAN
    heads = quarter // HEAD_DIM
    group = SPAN * toks
    kv = jnp.swapaxes(keys_values[0], 0, 1)
    dma = pltpu.SemaphoreType.DMA
    any_spec = pl.BlockSpec(memory_space=pl.ANY)
    vm = pl.BlockSpec(memory_space=pltpu.VMEM)
    near = dma((SPAN, heads))
    line = dma((heads,))
    sides = dma((fsdp, heads))
    levels = dma((planes, heads))
    dq, out_kv, out_w = pl.pallas_call(
        functools.partial(layer_kernel, planes, fsdp),
        out_shape=(
            jax.ShapeDtypeStruct((toks, width), BF16),
            jax.ShapeDtypeStruct((2, toks, width), BF16),
            jax.ShapeDtypeStruct((own_rows, width), F32),
        ),
        in_specs=[any_spec] * 4,
        out_specs=(any_spec, any_spec, vm),
        scratch_shapes=[
            pltpu.VMEM((group, quarter), BF16),
            pltpu.VMEM((2, 2 * group, quarter), BF16),
            pltpu.VMEM((group, model), BF16),
            pltpu.VMEM((model, group), BF16),
            pltpu.VMEM((model, quarter), BF16),
            pltpu.VMEM((group, quarter), BF16),
            pltpu.VMEM((group, quarter), BF16),
            pltpu.VMEM((heads * SPAN, toks, group + toks), BF16),
            pltpu.VMEM((SPAN, toks, group + toks), F32),
            pltpu.VMEM((group, quarter), BF16),
            pltpu.VMEM((2, 2 * group, quarter), F32),
            pltpu.VMEM((2, group, quarter), BF16),
            pltpu.VMEM((2, group, quarter), BF16),
            pltpu.VMEM((2, group, quarter), BF16),
            pltpu.VMEM((fsdp, model // fsdp, quarter), BF16),
            pltpu.VMEM((fsdp, model // fsdp, quarter), BF16),
            pltpu.VMEM((planes, SPAN * own_rows, quarter), BF16),
            pltpu.VMEM((planes, SPAN * own_rows, quarter), BF16),
            pltpu.VMEM((SPAN, own_rows, quarter), BF16),
            pltpu.VMEM((SPAN, own_rows, quarter), BF16),
            dma((4,)), near, near, near, near, dma((SPAN,)), dma((SPAN,)), sides, sides, near, near,
            near, near, line, line, near, near, sides, sides, levels, levels, near, near,
        ],
        compiler_params=pltpu.CompilerParams(collective_id=0, has_side_effects=True),
        name="layer",
    )(queries[0], kv, upstream[0], out_weight)
    return dq[None], jnp.swapaxes(out_kv, 0, 1)[None], out_w


def solution(mesh):
    return jax.shard_map(
        shards,
        mesh=mesh,
        in_specs=(
            P("fsdp", "ctx", None),
            P("fsdp", "ctx", None, None),
            P("fsdp", "ctx", None),
            P("fsdp", None),
        ),
        out_specs=(P("fsdp", "ctx", None), P("fsdp", "ctx", None, None), P(("ctx", "fsdp"), None)),
        check_vma=False,
    )
```

time: 132 us -> 94.4 us (0.72)
  the two profiles are of different devices: /device:TPU:4 before, /device:TPU:0 now
where the time goes in v1:
time: 94.4 us; the launch traced here: 94.1 us
  Pallas kernels  83.9 us (89%)
  local copies, waits for them, and re-layouts  9.57 us (10%)
    pallas_call x1, Pallas kernels, shards(): pl.pallas_call(functools.partial(layer_kernel, planes, fsdp), out_shape=(...  83.9 us
    unnamed x4, local copies, waits for them, and re-layouts  9.57 us

profile of v1, /device:TPU:0, one launch (start us, length us, event | category | flops | bytes accessed | tf_op | source)
XLA Modules:
  0.0 94.1 jit_solution(17001834487290006206)
XLA Ops:
  0.6 2.5 %copy.10 = bf16[1,128,2,2048]{3,1,2,0:T(8,128)(2,1)} copy(bf16[1,128,2,2048]{3,2,1,0:T(2,128)(2,1)} %param.5) | data formatting | bytes 2097152 | tf_op args[1]
  3.2 83.9 %layer.1 = (bf16[128,2048]{1,0:T(8,128)(2,1)}, bf16[2,128,2048]{2,1,0:T(8,128)(2,1)}, f32[64,2048]{1,0:T(8,128)}) custom-call(bf16[128,2048]{1,0:T(8,128)(2,1)} %bitcast.13, bf16[2,128,2048]{2,1,0:T(8,128)(2,1)} %bitcast.11, bf16[128,2048]{1,0:T(8,128)(2,1)} %bitcast.14, bf16[1024,2048]{1,0:T(8,128)(2,1)} %weight.1), custom_call_target="tpu_custom_call" | custom-call | tf_op jit(solution)/shard_map/layer/pallas_call | solution.py:424
  87.1 3.3 %copy.8 = bf16[1,128,2,2048]{3,2,1,0:T(2,128)(2,1)} copy(bf16[1,128,2,2048]{3,1,2,0:T(8,128)(2,1)} %bitcast.12) | data formatting | bytes 2097152
  90.4 1.9 %copy.13 = bf16[1,128,2048]{2,1,0:T(8,128)(2,1)} copy(bf16[1,128,2048]{2,1,0:T(8,128)(2,1)} %bitcast.15) | data formatting | bytes 1048576
  92.2 1.9 %copy.14 = f32[64,2048]{1,0:T(8,128)} copy(f32[64,2048]{1,0:T(8,128)} %get-tuple-element.17) | data formatting | bytes 1048576

commit v2 on v1

--- a/solution.py
+++ b/solution.py
@@ -27,9 +27,9 @@
     q_in, kv_in, up_in, weight,
     dq_out, kv_out, out_w,
     q, kv, up, up_t, w, ga, att, low, bias, dq, dkv, dprev, dprev_in, dsum,
-    gw_out, gw_in, zw_out, zw_in, fin_out, fin_in,
+    gw_out, gw_in, zw_out, pin, tin, fin_out, fin_in,
     own_sem, kv_s, kv_r, q_s, q_r, u_s, u_r, w_s, w_r, kz_s, kz_r,
-    dq_s, dq_r, dz_s, dz_r, dk_s, dk_r, gx_s, gx_r, gz_s, gz_r, f_s, f_r,
+    dq_s, dq_r, dz_s, dz_r, dk_s, dk_r, gx_s, gx_r, pin_s, pin_r, tin_s, tin_r, f_s, f_r,
 ):
     toks = q_in.shape[0]
     depth = weight.shape[0]
@@ -168,15 +168,25 @@
         here = gw_in.at[df, :, head(c)]
         remote(here, here, gx_s.at[df, c], gx_r.at[df, c], dev(p, r, side(df))).wait_recv()
 
-    def gz_copy(dp, c):
-        return remote(
-            zw_out.at[level(dp), :, head(c)], zw_in.at[planes - dp, :, head(c)], gz_s.at[dp, c], gz_r.at[planes - dp, c],
-            dev(level(dp), r, f),
-        )
-
-    def gz_came(dp, c):
-        here = zw_in.at[dp, :, head(c)]
-        remote(here, here, gz_s.at[dp, c], gz_r.at[dp, c], dev(level(dp), r, f)).wait_recv()
+    lower = lax.rem(p, 2) == 0
+    partner = dev(p + 1 - 2 * lax.rem(p, 2), r, f)
+    group = lax.div(p, 2)
+
+    def to_partner(n):
+        return jnp.logical_or(jnp.logical_and(lower, n > p), jnp.logical_and(jnp.logical_not(lower), n < p))
+
+    def to_plane(n):
+        return jnp.logical_or(jnp.logical_and(lower, n < p), jnp.logical_and(jnp.logical_not(lower), n > p))
+
+    def pin_copy(n, c):
+        return remote(zw_out.at[n, :, head(c)], pin.at[n, :, head(c)], pin_s.at[n, c], pin_r.at[n, c], partner)
+
+    def tin_copy(n, c):
+        return remote(zw_out.at[n, :, head(c)], tin.at[group, :, head(c)], tin_s.at[n, c], tin_r.at[group, c], dev(n, r, f))
+
+    def tin_came(k, c):
+        here = tin.at[k, :, head(c)]
+        remote(here, here, tin_s.at[0, c], tin_r.at[k, c], partner).wait_recv()
 
     def f_copy(d, c):
         return remote(fin_out.at[peer[d], :, head(c)], fin_in.at[r, :, head(c)], f_s.at[d, c], f_r.at[d, c], near(d))
@@ -193,18 +203,32 @@
         for d in around:
             q_copy(d, c).start()
 
-    for c in range(heads):
+    def halo(c):
         @pl.when(not_last)
-        def _(c=c):
+        def _():
             kz_copy(0, c).start()
 
+    def columns(c):
         for df in range(1, fsdp):
             w_copy(df, c).start()
-        spread(c)
-        if c == 1:
-            up_copy(2).start()
-            up_copy(1).start()
-
+
+    def lift():
+        up_copy(2).start()
+        up_copy(1).start()
+
+    spread(0)
+    lift()
+    columns(1)
+    spread(2)
+    spread(3)
+    columns(0)
+    columns(2)
+    columns(3)
+    halo(1)
+    halo(0)
+    spread(1)
+    halo(3)
+    halo(2)
     row = lax.broadcasted_iota(jnp.int32, (toks, keys), 0)
     col = lax.broadcasted_iota(jnp.int32, (toks, keys), 1)
     for b in range(SPAN):
@@ -280,36 +304,30 @@
             dk_copy(d, c).start()
         own_dk(c).start()
 
-    pair = 2 * HEAD_DIM
-
-    def project(g):
-        for c in (2 * g, 2 * g + 1):
+    def project(c, d):
+        if d == 0:
             for df in range(1, fsdp):
                 w_came(df, c)
-        for b in range(SPAN):
-            block = pl.ds(b * toks, toks)
-            ga[block, g * pair : (g + 1) * pair] = jnp.dot(
-                up[block, :], w[:, g * pair : (g + 1) * pair], preferred_element_type=F32
-            ).astype(BF16)
+        ga[rows(peer[d]), head(c)] = jnp.dot(up[rows(peer[d]), :], w[:, head(c)], preferred_element_type=F32).astype(BF16)
+
+    def turn(d):
+        up_t[:, rows(peer[d])] = up[rows(peer[d]), :].T
 
     tile = plane_toks
     unit = fsdp * own_rows
 
-    def weigh(g):
-        cols = slice(g * pair, (g + 1) * pair)
-
+    def weigh(c):
         def step(t, _):
-            value = jnp.dot(up_t[pl.ds(pl.multiple_of(t * tile, tile), tile), :], att[:, cols], preferred_element_type=F32)
-            value = value.reshape(tile // unit, fsdp, own_rows, pair)
+            value = jnp.dot(up_t[pl.ds(pl.multiple_of(t * tile, tile), tile), :], att[:, head(c)], preferred_element_type=F32)
+            value = value.reshape(tile // unit, fsdp, own_rows, HEAD_DIM)
             part = tile // fsdp
             for n in range(fsdp):
-                gw_out[n, pl.ds(pl.multiple_of(t * part, part), part), cols] = value[:, n].reshape(part, pair).astype(BF16)
+                gw_out[n, pl.ds(pl.multiple_of(t * part, part), part), head(c)] = value[:, n].reshape(part, HEAD_DIM).astype(BF16)
             return 0
 
         lax.fori_loop(0, up_t.shape[0] // tile, step, 0)
-        for c in (2 * g, 2 * g + 1):
-            for df in range(1, fsdp):
-                gx_copy(df, c).start()
+        for df in range(1, fsdp):
+            gx_copy(df, c).start()
 
     def merge(c):
         total = gw_out[f, :, head(c)].astype(F32)
@@ -318,14 +336,26 @@
             total = total + gw_in[df, :, head(c)].astype(F32)
         for n in range(planes):
             zw_out[n, :, head(c)] = total[n * plane_rows : (n + 1) * plane_rows].astype(BF16)
-        for dp in range(1, planes):
-            gz_copy(dp, c).start()
+        for n in range(planes):
+            @pl.when(to_partner(n))
+            def _(n=n):
+                pin_copy(n, c).start()
+
+    def relay(c):
+        for n in range(planes):
+            @pl.when(to_plane(n))
+            def _(n=n):
+                pin_copy(n, c).wait_recv()
+                zw_out[n, :, head(c)] = (zw_out[n, :, head(c)].astype(F32) + pin[n, :, head(c)].astype(F32)).astype(BF16)
+                tin_copy(n, c).start()
 
     def total_up(c):
-        total = zw_out[p, :, head(c)].astype(F32)
-        for dp in range(1, planes):
-            gz_came(dp, c)
-            total = total + zw_in[dp, :, head(c)].astype(F32)
+        pin_copy(p, c).wait_recv()
+        total = zw_out[p, :, head(c)].astype(F32) + pin[p, :, head(c)].astype(F32)
+        for dk in range(1, planes // 2):
+            k = lax.rem(group + dk, planes // 2)
+            tin_came(k, c)
+            total = total + tin[k, :, head(c)].astype(F32)
         for n in range(SPAN):
             fin_out[n, :, head(c)] = total[n * own_rows : (n + 1) * own_rows].astype(BF16)
         for d in (2, 3, 1):
@@ -338,45 +368,77 @@
         for d in around:
             out_w[:, wide_head(peer[d], c)] = fin_in[peer[d], :, head(c)].astype(F32)
 
+    def settle():
+        for copy in own_copies:
+            copy.wait()
+        up_came(1)
+        turn(0)
+        turn(1)
+
+    def lift_on():
+        up_came(2)
+        up_copy(3).start()
+        turn(2)
+
+    def lift_end():
+        up_came(3)
+        turn(3)
+
+    def project_chip(c):
+        project(c, 0)
+        project(c, 1)
+
+    def project_rest(c):
+        project(c, 2)
+        project(c, 3)
+
+    settle()
     forward(0)
-    forward(1)
-    for copy in own_copies:
-        copy.wait()
+    project_chip(0)
+    lift_on()
     attend(0)
-    attend(1)
-    up_came(2)
-    up_copy(3).start()
-    up_came(1)
-    up_came(3)
-    for i in range(up_t.shape[0] // tile):
-        up_t[i * tile : (i + 1) * tile, :] = up[:, i * tile : (i + 1) * tile].T
+    lift_end()
+    project_rest(0)
+    forward(2)
+    project_chip(1)
+    backward(0)
     weigh(0)
-    project(0)
-    backward(0)
-    forward(2)
-    backward(1)
-    merge(0)
+    project_rest(1)
+    project_chip(2)
+    project_rest(2)
     forward(3)
     attend(2)
-    project(1)
+    backward(2)
+    weigh(2)
+    project_chip(3)
+    project_rest(3)
+    forward(1)
     collect(0)
+    merge(0)
+    attend(3)
+    weigh(3)
+    attend(1)
+    relay(0)
+    merge(2)
+    weigh(1)
+    backward(3)
+    relay(2)
     merge(1)
-    attend(3)
-    weigh(1)
     total_up(0)
-    backward(2)
+    collect(2)
+    total_up(2)
+    relay(1)
+    merge(3)
+    backward(1)
+    relay(3)
+    total_up(1)
+    collect(3)
+    finish(0)
     collect(1)
-    total_up(1)
-    backward(3)
-    merge(2)
-    collect(2)
-    merge(3)
-    total_up(2)
-    collect(3)
+    finish(1)
+    finish(2)
     total_up(3)
-    for c in range(heads):
-        finish(c)
-
+    finish(3)
     for c in range(heads):
         for d in around:
             dq_came(d, c)
@@ -388,8 +450,14 @@
         for df in range(1, fsdp):
             w_copy(df, c).wait_send()
             gx_copy(df, c).wait_send()
-        for dp in range(1, planes):
-            gz_copy(dp, c).wait_send()
+        for n in range(planes):
+            @pl.when(to_partner(n))
+            def _(n=n, c=c):
+                pin_copy(n, c).wait_send()
+
+            @pl.when(to_plane(n))
+            def _(n=n, c=c):
+                tin_copy(n, c).wait_send()
 
         @pl.when(not_last)
         def _(c=c):
@@ -449,10 +517,11 @@
             pltpu.VMEM((fsdp, model // fsdp, quarter), BF16),
             pltpu.VMEM((planes, SPAN * own_rows, quarter), BF16),
             pltpu.VMEM((planes, SPAN * own_rows, quarter), BF16),
+            pltpu.VMEM((planes // 2, SPAN * own_rows, quarter), BF16),
             pltpu.VMEM((SPAN, own_rows, quarter), BF16),
             pltpu.VMEM((SPAN, own_rows, quarter), BF16),
             dma((4,)), near, near, near, near, dma((SPAN,)), dma((SPAN,)), sides, sides, near, near,
-            near, near, line, line, near, near, sides, sides, levels, levels, near, near,
+            near, near, line, line, near, near, sides, sides, levels, levels, levels, dma((planes // 2, heads)), near, near,
         ],
         compiler_params=pltpu.CompilerParams(collective_id=0, has_side_effects=True),
         name="layer",

time: 94.4 us -> 89.3 us (0.946)
  Pallas kernels: 83.9 us -> 78.8 us
    pallas_call x1, Pallas kernels: 83.9 us -> 78.8 us  [shards(): pl.pallas_call(functools.partial(layer_kernel, planes, fsdp), out_shape=(...]
where the time goes in v2:
time: 89.3 us; the launch traced here: 89.1 us
  Pallas kernels  78.8 us (88%)
  local copies, waits for them, and re-layouts  9.57 us (11%)
    pallas_call x1, Pallas kernels, shards(): pl.pallas_call(functools.partial(layer_kernel, planes, fsdp), out_shape=(...  78.8 us
    unnamed x4, local copies, waits for them, and re-layouts  9.57 us

profile of v2, /device:TPU:0, one launch (start us, length us, event | category | flops | bytes accessed | tf_op | source)
XLA Modules:
  0.0 89.1 jit_solution(16435489848089320423)
XLA Ops:
  0.6 2.5 %copy.10 = bf16[1,128,2,2048]{3,1,2,0:T(8,128)(2,1)} copy(bf16[1,128,2,2048]{3,2,1,0:T(2,128)(2,1)} %param.5) | data formatting | bytes 2097152 | tf_op args[1]
  3.2 78.8 %layer.1 = (bf16[128,2048]{1,0:T(8,128)(2,1)}, bf16[2,128,2048]{2,1,0:T(8,128)(2,1)}, f32[64,2048]{1,0:T(8,128)}) custom-call(bf16[128,2048]{1,0:T(8,128)(2,1)} %bitcast.13, bf16[2,128,2048]{2,1,0:T(8,128)(2,1)} %bitcast.11, bf16[128,2048]{1,0:T(8,128)(2,1)} %bitcast.14, bf16[1024,2048]{1,0:T(8,128)(2,1)} %weight.1), custom_call_target="tpu_custom_call" | custom-call | tf_op jit(solution)/shard_map/layer/pallas_call | solution.py:492
  82.0 3.3 %copy.8 = bf16[1,128,2,2048]{3,2,1,0:T(2,128)(2,1)} copy(bf16[1,128,2,2048]{3,1,2,0:T(8,128)(2,1)} %bitcast.12) | data formatting | bytes 2097152
  85.3 1.9 %copy.13 = bf16[1,128,2048]{2,1,0:T(8,128)(2,1)} copy(bf16[1,128,2048]{2,1,0:T(8,128)(2,1)} %bitcast.15) | data formatting | bytes 1048576
  87.2 1.9 %copy.14 = f32[64,2048]{1,0:T(8,128)} copy(f32[64,2048]{1,0:T(8,128)} %get-tuple-element.17) | data formatting | bytes 1048576

commit v3 on v2

--- a/solution.py
+++ b/solution.py
@@ -24,9 +24,9 @@
 
 def layer_kernel(
     planes, fsdp,
-    q_in, kv_in, up_in, weight,
+    q_in, kv_pairs, up_in, weight,
     dq_out, kv_out, out_w,
-    q, kv, up, up_t, w, ga, att, low, bias, dq, dkv, dprev, dprev_in, dsum,
+    kv_raw, kv_in, q, kv, up, up_t, w, ga, att, low, bias, dq, dkv, dprev, dprev_in, dsum,
     gw_out, gw_in, zw_out, pin, tin, fin_out, fin_in,
     own_sem, kv_s, kv_r, q_s, q_r, u_s, u_r, w_s, w_r, kz_s, kz_r,
     dq_s, dq_r, dz_s, dz_r, dk_s, dk_r, gx_s, gx_r, pin_s, pin_r, tin_s, tin_r, f_s, f_r,
@@ -81,8 +81,9 @@
     def w_rows(i):
         return pl.ds(pl.multiple_of(i * depth, depth), depth)
 
+    pairs_copy = pltpu.make_async_copy(kv_pairs, kv_raw, own_sem.at[0])
+    pairs_copy.start()
     own_copies = [
-        pltpu.make_async_copy(kv_in.at[:, :, quart(r)], kv.at[:, own_plane(r), :], own_sem.at[0]),
         pltpu.make_async_copy(q_in.at[:, quart(r)], q.at[rows(r), :], own_sem.at[1]),
         pltpu.make_async_copy(up_in, up.at[rows(r), :], own_sem.at[2]),
         pltpu.make_async_copy(weight.at[:, quart(r)], w.at[w_rows(f), :], own_sem.at[3]),
@@ -96,6 +97,9 @@
     targets += [dev(level(dp), r, f) for dp in range(1, planes)]
     for target in targets:
         pl.semaphore_signal(sem, inc=1, device_id=target, device_id_type=pl.DeviceIdType.MESH)
+    pairs_copy.wait()
+    for n in range(2):
+        kv_in[n] = kv_raw[:, n, :]
     pl.semaphore_wait(sem, len(targets))
 
     def kv_copy(d, c):
@@ -369,6 +373,7 @@
             out_w[:, wide_head(peer[d], c)] = fin_in[peer[d], :, head(c)].astype(F32)
 
     def settle():
+        kv[:, own_plane(r), :] = kv_in[:, :, quart(r)]
         for copy in own_copies:
             copy.wait()
         up_came(1)
@@ -472,6 +477,29 @@
         up_copy(d).wait_send()
 
 
+def hand_over_kernel(dq_in, kv_in, w_in, dq_out, kv_out, w_out):
+    dq_out[...] = dq_in[...]
+    w_out[...] = w_in[...]
+    for n in range(2):
+        kv_out[:, n, :] = kv_in[n]
+
+
+def hand_over(dq, kv, w):
+    toks, width = dq.shape
+    vm = pl.BlockSpec(memory_space=pltpu.VMEM)
+    return pl.pallas_call(
+        hand_over_kernel,
+        out_shape=(
+            jax.ShapeDtypeStruct(dq.shape, dq.dtype),
+            jax.ShapeDtypeStruct((toks, 2, width), kv.dtype),
+            jax.ShapeDtypeStruct(w.shape, w.dtype),
+        ),
+        in_specs=[vm] * 3,
+        out_specs=(vm,) * 3,
+        name="hand_over",
+    )(dq, kv, w)
+
+
 def shards(queries, keys_values, upstream, out_weight):
     seqs, toks, width = queries.shape
     ctx, fsdp = lax.axis_size("ctx"), lax.axis_size("fsdp")
@@ -481,7 +509,6 @@
     quarter = width // SPAN
     heads = quarter // HEAD_DIM
     group = SPAN * toks
-    kv = jnp.swapaxes(keys_values[0], 0, 1)
     dma = pltpu.SemaphoreType.DMA
     any_spec = pl.BlockSpec(memory_space=pl.ANY)
     vm = pl.BlockSpec(memory_space=pltpu.VMEM)
@@ -499,6 +526,8 @@
         in_specs=[any_spec] * 4,
         out_specs=(any_spec, any_spec, vm),
         scratch_shapes=[
+            pltpu.VMEM((toks, 2, width), BF16),
+            pltpu.VMEM((2, toks, width), BF16),
             pltpu.VMEM((group, quarter), BF16),
             pltpu.VMEM((2, 2 * group, quarter), BF16),
             pltpu.VMEM((group, model), BF16),
@@ -525,8 +554,9 @@
         ],
         compiler_params=pltpu.CompilerParams(collective_id=0, has_side_effects=True),
         name="layer",
-    )(queries[0], kv, upstream[0], out_weight)
-    return dq[None], jnp.swapaxes(out_kv, 0, 1)[None], out_w
+    )(queries[0], keys_values[0], upstream[0], out_weight)
+    dq, out_kv, out_w = hand_over(dq, out_kv, out_w)
+    return dq[None], out_kv[None], out_w
 
 
 def solution(mesh):

time: 89.3 us -> 83.1 us (0.931)
  local copies, waits for them, and re-layouts: 9.57 us -> 0 us
  Pallas kernels: 78.8 us -> 82.3 us
    unnamed x4 -> x0, local copies, waits for them, and re-layouts: 9.57 us -> none
    pallas_call x0 -> x1, Pallas kernels: none -> 3.2 us  [hand_over(): pl.pallas_call(hand_over_kernel, out_shape=(jax.ShapeDtypeStruct(dq.shape...]
where the time goes in v3:
time: 83.1 us; the launch traced here: 82.9 us
  Pallas kernels  82.3 us (99%)
    pallas_call x1, Pallas kernels, shards(): pl.pallas_call(functools.partial(layer_kernel, planes, fsdp), out_shape=(...  79.1 us
    pallas_call x1, Pallas kernels, hand_over(): pl.pallas_call(hand_over_kernel, out_shape=(jax.ShapeDtypeStruct(dq.shape...  3.2 us

profile of v3, /device:TPU:0, one launch (start us, length us, event | category | flops | bytes accessed | tf_op | source)
XLA Modules:
  0.0 82.9 jit_solution(7021313190362293962)
XLA Ops:
  0.6 79.1 %layer.1 = (bf16[128,2048]{1,0:T(8,128)(2,1)}, bf16[2,128,2048]{2,1,0:T(8,128)(2,1)}, f32[64,2048]{1,0:T(8,128)}) custom-call(bf16[128,2048]{1,0:T(8,128)(2,1)} %bitcast.6, bf16[128,2,2048]{2,1,0:T(2,128)(2,1)} %bitcast.5, bf16[128,2048]{1,0:T(8,128)(2,1)} %bitcast.7, bf16[1024,2048]{1,0:T(8,128)(2,1)} %weight.1), custom_call_target="tpu_custom_call" | custom-call | tf_op jit(solution)/shard_map/layer/pallas_call | solution.py:519
  79.7 3.2 %hand_over.1 = (bf16[128,2048]{1,0:T(8,128)(2,1)}, bf16[128,2,2048]{2,1,0:T(2,128)(2,1)}, f32[64,2048]{1,0:T(8,128)}) custom-call(bf16[128,2048]{1,0:T(8,128)(2,1)} %get-tuple-element.9.dq_in, bf16[2,128,2048]{2,1,0:T(8,128)(2,1)} %get-tuple-element.10.kv_in, f32[64,2048]{1,0:T(8,128)} %get-tuple-element.11.w_in), custom_call_target="tpu_custom_call" | custom-call | tf_op jit(solution)/shard_map/hand_over/pallas_call | solution.py:490

commit v4 on v3

--- a/solution.py
+++ b/solution.py
@@ -26,14 +26,15 @@
     planes, fsdp,
     q_in, kv_pairs, up_in, weight,
     dq_out, kv_out, out_w,
-    kv_raw, kv_in, q, kv, up, up_t, w, ga, att, low, bias, dq, dkv, dprev, dprev_in, dsum,
+    kv_raw, kv_in, q, kv, up, up_t, w, ga, att, low, bias, dq, dkv, dsum, q_next, ga_next, stats, stats_next,
     gw_out, gw_in, zw_out, pin, tin, fin_out, fin_in,
     own_sem, kv_s, kv_r, q_s, q_r, u_s, u_r, w_s, w_r, kz_s, kz_r,
-    dq_s, dq_r, dz_s, dz_r, dk_s, dk_r, gx_s, gx_r, pin_s, pin_r, tin_s, tin_r, f_s, f_r,
+    dq_s, dq_r, dk_s, dk_r, qz_s, qz_r, gz_s, gz_r, st_s, st_r, gx_s, gx_r, pin_s, pin_r, tin_s, tin_r, f_s, f_r,
 ):
     toks = q_in.shape[0]
     depth = weight.shape[0]
     width = weight.shape[1]
+    width_up = up_in.shape[1] // 2
     quarter = width // SPAN
     heads = quarter // HEAD_DIM
     plane_toks = SPAN * toks
@@ -116,15 +117,16 @@
         here = q.at[rows(peer[d]), head(c)]
         remote(here, here, q_s.at[d, c], q_r.at[d, c], near(d)).wait_recv()
 
-    def up_copy(d):
+    def up_copy(d, h):
+        cols = slice(h * width_up, (h + 1) * width_up)
         if d == 3:
-            here = up.at[rows(peer[2]), :]
-            return remote(here, here, u_s.at[3], u_r.at[3], near(1))
-        return remote(up_in, up.at[rows(r), :], u_s.at[d], u_r.at[d], near(d))
-
-    def up_came(d):
-        here = up.at[rows(peer[d]), :]
-        remote(here, here, u_s.at[d], u_r.at[d], near(d)).wait_recv()
+            here = up.at[rows(peer[2]), cols]
+            return remote(here, here, u_s.at[3, h], u_r.at[3, h], near(1))
+        return remote(up_in.at[:, cols], up.at[rows(r), cols], u_s.at[d, h], u_r.at[d, h], near(d))
+
+    def up_came(d, h):
+        here = up.at[rows(peer[d]), h * width_up : (h + 1) * width_up]
+        remote(here, here, u_s.at[d, h], u_r.at[d, h], near(d)).wait_recv()
 
     def w_copy(df, c):
         return remote(
@@ -139,28 +141,47 @@
         src = kv_in.at[:, :, wide_head(r, c)] if d == 0 else kv.at[:, own_plane(peer[d]), head(c)]
         return remote(src, kv.at[:, rows(peer[d]), head(c)], kz_s.at[d, c], kz_r.at[d, c], dev(p + 1, r, f))
 
-    def dq_copy(d, c):
-        return remote(dq.at[rows(peer[d]), head(c)], dq_out.at[:, wide_head(r, c)], dq_s.at[d, c], dq_r.at[d, c], near(d))
+    def block_head(ref, lead, j, c):
+        return ref.at[lead + (slice(j * toks, (j + 1) * toks), head(c))]
+
+    def dq_copy(j, c):
+        return remote(block_head(dq, (), j, c), dq_out.at[:, wide_head(r, c)], dq_s.at[j, c], dq_r.at[r, c], dev(p, j, f))
 
     def dq_came(d, c):
         here = dq_out.at[:, wide_head(peer[d], c)]
-        remote(here, here, dq_s.at[d, c], dq_r.at[d, c], near(d)).wait_recv()
-
-    def own_dq(c):
-        return pltpu.make_async_copy(dq.at[rows(r), head(c)], dq_out.at[:, wide_head(r, c)], dq_s.at[0, c])
-
-    def dz_copy(c):
-        return remote(dprev.at[:, :, head(c)], dprev_in.at[:, :, head(c)], dz_s.at[c], dz_r.at[c], dev(p - 1, r, f))
-
-    def dk_copy(d, c):
-        return remote(dsum.at[:, rows(peer[d]), head(c)], kv_out.at[:, :, wide_head(r, c)], dk_s.at[d, c], dk_r.at[d, c], near(d))
+        remote(here, here, dq_s.at[0, c], dq_r.at[peer[d], c], near(d)).wait_recv()
+
+    def own_dq(j, c):
+        return pltpu.make_async_copy(block_head(dq, (), j, c), dq_out.at[:, wide_head(r, c)], dq_s.at[j, c])
+
+    def qz_copy(d, c):
+        src = q_in.at[:, wide_head(r, c)] if d == 0 else q.at[rows(peer[d]), head(c)]
+        return remote(src, q_next.at[rows(peer[d]), head(c)], qz_s.at[d, c], qz_r.at[d, c], dev(p - 1, r, f))
+
+    def ga_copy(c):
+        return remote(ga.at[:, head(c)], ga_next.at[:, head(c)], gz_s.at[c], gz_r.at[c], dev(p - 1, r, f))
+
+    def stats_copy(c):
+        return remote(stats.at[c], stats_next.at[c], st_s.at[c], st_r.at[c], dev(p - 1, r, f))
+
+    def dk_copy(j, c):
+        return remote(block_head(dsum, (slice(None),), j, c), kv_out.at[:, :, wide_head(r, c)], dk_s.at[j, c], dk_r.at[r, c], dev(p, j, f))
 
     def dk_came(d, c):
         here = kv_out.at[:, :, wide_head(peer[d], c)]
-        remote(here, here, dk_s.at[d, c], dk_r.at[d, c], near(d)).wait_recv()
-
-    def own_dk(c):
-        return pltpu.make_async_copy(dsum.at[:, rows(r), head(c)], kv_out.at[:, :, wide_head(r, c)], dk_s.at[0, c])
+        remote(here, here, dk_s.at[0, c], dk_r.at[peer[d], c], near(d)).wait_recv()
+
+    def own_dk(j, c):
+        return pltpu.make_async_copy(block_head(dsum, (slice(None),), j, c), kv_out.at[:, :, wide_head(r, c)], dk_s.at[j, c])
+
+    def hand(j, own, other):
+        @pl.when(r == j)
+        def _():
+            own()
+
+        @pl.when(r != j)
+        def _():
+            other()
 
     def gx_copy(df, c):
         return remote(
@@ -207,6 +228,10 @@
         for d in around:
             q_copy(d, c).start()
 
+        @pl.when(not_first)
+        def _():
+            qz_copy(0, c).start()
+
     def halo(c):
         @pl.when(not_last)
         def _():
@@ -217,28 +242,31 @@
             w_copy(df, c).start()
 
     def lift():
-        up_copy(2).start()
-        up_copy(1).start()
-
+        for h in range(2):
+            up_copy(2, h).start()
+        for h in range(2):
+            up_copy(1, h).start()
+
+    columns(1)
+    halo(2)
+    spread(2)
+    halo(0)
+    lift()
     spread(0)
-    lift()
-    columns(1)
-    spread(2)
+    columns(3)
+    columns(2)
     spread(3)
+    halo(3)
     columns(0)
-    columns(2)
-    columns(3)
     halo(1)
-    halo(0)
     spread(1)
-    halo(3)
-    halo(2)
     row = lax.broadcasted_iota(jnp.int32, (toks, keys), 0)
     col = lax.broadcasted_iota(jnp.int32, (toks, keys), 1)
     for b in range(SPAN):
         first = jnp.where(not_first, 0, plane_toks - b * toks)
         bias[b] = jnp.where((col > row) & (col <= row + plane_toks) & (col >= first), 0.0, NEGATIVE)
     dkv[...] = jnp.zeros(dkv.shape, F32)
+    stats[...] = jnp.zeros(stats.shape, F32)
 
     @pl.when(p == 0)
     def _():
@@ -252,13 +280,23 @@
             def _(d=d):
                 kz_copy(d, c).start()
 
+    def forward_q(c):
+        for d in around:
+            q_came(d, c)
+
+            @pl.when(not_first)
+            def _(d=d):
+                qz_copy(d, c).start()
+
+    diagonal = lax.broadcasted_iota(jnp.int32, (toks, toks), 0) == lax.broadcasted_iota(jnp.int32, (toks, toks), 1)
+
+    def as_row(column):
+        return jnp.sum(jnp.where(diagonal, column, 0.0), axis=0, keepdims=True)
+
     def window(b):
         return pl.ds(b * toks, keys)
 
     def attend(c):
-        for d in around:
-            q_came(d, c)
-
         @pl.when(not_first)
         def _():
             for d in range(SPAN):
@@ -268,10 +306,25 @@
         for b in range(SPAN):
             block = pl.ds(b * toks, toks)
             scores = lax.dot_general(q[block, head(c)], kv[0, window(b), head(c)], NT, preferred_element_type=F32) * inv_root + bias[b]
-            lifted = jnp.exp(scores - jnp.max(scores, axis=-1, keepdims=True))
-            prob = (lifted * (1.0 / jnp.sum(lifted, axis=-1, keepdims=True))).astype(BF16)
+            top = jnp.max(scores, axis=-1, keepdims=True)
+            lifted = jnp.exp(scores - top)
+            mass = jnp.sum(lifted, axis=-1, keepdims=True)
+            stats[c, 0:1, block] = as_row(top + jnp.log(mass))
+            prob = (lifted * (1.0 / mass)).astype(BF16)
             low[c * SPAN + b] = prob
             att[block, head(c)] = jnp.dot(prob, kv[1, window(b), head(c)], preferred_element_type=F32).astype(BF16)
+
+    def center_of(block, c):
+        return jnp.sum(ga[block, head(c)].astype(F32) * att[block, head(c)].astype(F32), axis=-1, keepdims=True)
+
+    def send_down(c):
+        @pl.when(not_first)
+        def _():
+            for b in range(SPAN):
+                block = pl.ds(b * toks, toks)
+                stats[c, 1:2, block] = as_row(center_of(block, c))
+            ga_copy(c).start()
+            stats_copy(c).start()
 
     def backward(c):
         for b in range(SPAN):
@@ -280,33 +333,42 @@
             prob = low[c * SPAN + b]
             k = kv[0, window(b), head(c)]
             products = lax.dot_general(g, kv[1, window(b), head(c)], NT, preferred_element_type=F32)
-            center = jnp.sum(g.astype(F32) * att[block, head(c)].astype(F32), axis=-1, keepdims=True)
-            ds = (prob.astype(F32) * (products - center)).astype(BF16)
+            ds = (prob.astype(F32) * (products - center_of(block, c))).astype(BF16)
             dq[block, head(c)] = (jnp.dot(ds, k, preferred_element_type=F32) * inv_root).astype(BF16)
-            dkv[0, window(b), head(c)] += lax.dot_general(ds, q[block, head(c)], TN, preferred_element_type=F32) * inv_root
-            dkv[1, window(b), head(c)] += lax.dot_general(prob, g, TN, preferred_element_type=F32)
-        for d in (2, 3, 1):
-            dq_copy(d, c).start()
-        own_dq(c).start()
-        dprev[:, :, head(c)] = dkv[:, :plane_toks, head(c)].astype(BF16)
-
-        @pl.when(not_first)
-        def _():
-            dz_copy(c).start()
-
-    def collect(c):
+            seen = slice(plane_toks - b * toks, keys)
+            mine = slice(0, (b + 1) * toks)
+            dkv[0, mine, head(c)] += lax.dot_general(ds[:, seen], q[block, head(c)], TN, preferred_element_type=F32) * inv_root
+            dkv[1, mine, head(c)] += lax.dot_general(prob[:, seen], g, TN, preferred_element_type=F32)
+        for j in range(SPAN):
+            hand(j, lambda: own_dq(j, c).start(), lambda: dq_copy(j, c).start())
+
+    def next_plane(c):
         @pl.when(not_last)
         def _():
-            dz_copy(c).wait_recv()
-            dsum[:, :, head(c)] = (dkv[:, plane_toks:, head(c)] + dprev_in[:, :, head(c)].astype(F32)).astype(BF16)
-
-        @pl.when(p == planes - 1)
-        def _():
-            dsum[:, :, head(c)] = dkv[:, plane_toks:, head(c)].astype(BF16)
-
-        for d in (2, 3, 1):
-            dk_copy(d, c).start()
-        own_dk(c).start()
+            for d in range(SPAN):
+                here = q_next.at[rows(peer[d]), head(c)]
+                remote(here, here, qz_s.at[d, c], qz_r.at[d, c], near(1)).wait_recv()
+            ga_copy(c).wait_recv()
+            stats_copy(c).wait_recv()
+            for b in range(SPAN):
+                block = pl.ds(b * toks, toks)
+                count = plane_toks - b * toks
+                mine = slice(b * toks, plane_toks)
+                seen = slice(plane_toks + b * toks, 2 * plane_toks)
+                shape = (count, toks)
+                visible = lax.broadcasted_iota(jnp.int32, shape, 0) > lax.broadcasted_iota(jnp.int32, shape, 1)
+                qn, gn = q_next[block, head(c)], ga_next[block, head(c)]
+                scores = lax.dot_general(kv[0, seen, head(c)], qn, NT, preferred_element_type=F32) * inv_root
+                prob = jnp.exp(jnp.where(visible, scores - stats_next[c, 0:1, block], NEGATIVE))
+                products = lax.dot_general(kv[1, seen, head(c)], gn, NT, preferred_element_type=F32)
+                ds = (prob * (products - stats_next[c, 1:2, block])).astype(BF16)
+                dkv[0, mine, head(c)] += jnp.dot(ds, qn, preferred_element_type=F32) * inv_root
+                dkv[1, mine, head(c)] += jnp.dot(prob.astype(BF16), gn, preferred_element_type=F32)
+
+    def return_kv(c):
+        dsum[:, :, head(c)] = dkv[:, :, head(c)].astype(BF16)
+        for j in range(SPAN):
+            hand(j, lambda: own_dk(j, c).start(), lambda: dk_copy(j, c).start())
 
     def project(c, d):
         if d == 0:
@@ -376,17 +438,19 @@
         kv[:, own_plane(r), :] = kv_in[:, :, quart(r)]
         for copy in own_copies:
             copy.wait()
-        up_came(1)
+        for h in range(2):
+            up_came(1, h)
         turn(0)
         turn(1)
 
-    def lift_on():
-        up_came(2)
-        up_copy(3).start()
+    def lift_on(h):
+        up_came(2, h)
+        up_copy(3, h).start()
+
+    def lift_end():
         turn(2)
-
-    def lift_end():
-        up_came(3)
+        for h in range(2):
+            up_came(3, h)
         turn(3)
 
     def project_chip(c):
@@ -398,60 +462,74 @@
         project(c, 3)
 
     settle()
+    lift_on(0)
+    forward(2)
+    lift_on(1)
+    forward_q(2)
+    attend(2)
+    project_chip(2)
+    lift_end()
+    project_rest(2)
     forward(0)
+    send_down(2)
+    weigh(2)
+    forward_q(0)
+    forward(3)
     project_chip(0)
-    lift_on()
+    project_rest(0)
+    forward_q(3)
     attend(0)
-    lift_end()
-    project_rest(0)
-    forward(2)
+    send_down(0)
     project_chip(1)
-    backward(0)
-    weigh(0)
-    project_rest(1)
-    project_chip(2)
-    project_rest(2)
-    forward(3)
-    attend(2)
-    backward(2)
-    weigh(2)
     project_chip(3)
     project_rest(3)
     forward(1)
-    collect(0)
+    weigh(0)
+    forward_q(1)
+    attend(3)
+    merge(2)
+    weigh(3)
+    send_down(3)
+    attend(1)
+    next_plane(2)
+    project_rest(1)
     merge(0)
-    attend(3)
-    weigh(3)
-    attend(1)
+    backward(2)
+    send_down(1)
+    return_kv(2)
+    backward(0)
+    weigh(1)
+    next_plane(0)
+    return_kv(0)
+    relay(2)
+    backward(3)
+    merge(3)
     relay(0)
-    merge(2)
-    weigh(1)
-    backward(3)
-    relay(2)
+    next_plane(3)
+    return_kv(3)
+    next_plane(1)
     merge(1)
+    relay(3)
     total_up(0)
-    collect(2)
+    backward(1)
+    finish(0)
+    return_kv(1)
     total_up(2)
     relay(1)
-    merge(3)
-    backward(1)
-    relay(3)
+    total_up(3)
     total_up(1)
-    collect(3)
-    finish(0)
-    collect(1)
+    finish(3)
+    finish(2)
     finish(1)
-    finish(2)
-    total_up(3)
-    finish(3)
     for c in range(heads):
         for d in around:
             dq_came(d, c)
             dk_came(d, c)
-            for copy in (kv_copy(d, c), q_copy(d, c), dq_copy(d, c), dk_copy(d, c), f_copy(d, c)):
+            for copy in (kv_copy(d, c), q_copy(d, c), f_copy(d, c)):
                 copy.wait_send()
-        own_dq(c).wait()
-        own_dk(c).wait()
+        for j in range(SPAN):
+            hand(j, lambda: own_dq(j, c).wait(), lambda: dq_copy(j, c).wait_send())
+            hand(j, lambda: own_dk(j, c).wait(), lambda: dk_copy(j, c).wait_send())
         for df in range(1, fsdp):
             w_copy(df, c).wait_send()
             gx_copy(df, c).wait_send()
@@ -471,10 +549,14 @@
 
         @pl.when(not_first)
         def _(c=c):
-            dz_copy(c).wait_send()
+            for d in range(SPAN):
+                qz_copy(d, c).wait_send()
+            ga_copy(c).wait_send()
+            stats_copy(c).wait_send()
 
     for d in around:
-        up_copy(d).wait_send()
+        for h in range(2):
+            up_copy(d, h).wait_send()
 
 
 def hand_over_kernel(dq_in, kv_in, w_in, dq_out, kv_out, w_out):
@@ -513,7 +595,6 @@
     any_spec = pl.BlockSpec(memory_space=pl.ANY)
     vm = pl.BlockSpec(memory_space=pltpu.VMEM)
     near = dma((SPAN, heads))
-    line = dma((heads,))
     sides = dma((fsdp, heads))
     levels = dma((planes, heads))
     dq, out_kv, out_w = pl.pallas_call(
@@ -538,10 +619,12 @@
             pltpu.VMEM((heads * SPAN, toks, group + toks), BF16),
             pltpu.VMEM((SPAN, toks, group + toks), F32),
             pltpu.VMEM((group, quarter), BF16),
-            pltpu.VMEM((2, 2 * group, quarter), F32),
+            pltpu.VMEM((2, group, quarter), F32),
             pltpu.VMEM((2, group, quarter), BF16),
-            pltpu.VMEM((2, group, quarter), BF16),
-            pltpu.VMEM((2, group, quarter), BF16),
+            pltpu.VMEM((group, quarter), BF16),
+            pltpu.VMEM((group, quarter), BF16),
+            pltpu.VMEM((heads, 8, group), F32),
+            pltpu.VMEM((heads, 8, group), F32),
             pltpu.VMEM((fsdp, model // fsdp, quarter), BF16),
             pltpu.VMEM((fsdp, model // fsdp, quarter), BF16),
             pltpu.VMEM((planes, SPAN * own_rows, quarter), BF16),
@@ -549,8 +632,8 @@
             pltpu.VMEM((planes // 2, SPAN * own_rows, quarter), BF16),
             pltpu.VMEM((SPAN, own_rows, quarter), BF16),
             pltpu.VMEM((SPAN, own_rows, quarter), BF16),
-            dma((4,)), near, near, near, near, dma((SPAN,)), dma((SPAN,)), sides, sides, near, near,
-            near, near, line, line, near, near, sides, sides, levels, levels, levels, dma((planes // 2, heads)), near, near,
+            dma((4,)), near, near, near, near, dma((SPAN, 2)), dma((SPAN, 2)), sides, sides, near, near,
+            near, near, near, near, near, near, dma((heads,)), dma((heads,)), dma((heads,)), dma((heads,)), sides, sides, levels, levels, levels, dma((planes // 2, heads)), near, near,
         ],
         compiler_params=pltpu.CompilerParams(collective_id=0, has_side_effects=True),
         name="layer",

time: 83.1 us -> 79.4 us (0.955)
  Pallas kernels: 82.3 us -> 78.6 us
    pallas_call x1, Pallas kernels: 79.1 us -> 75.4 us  [shards(): pl.pallas_call(functools.partial(layer_kernel, planes, fsdp), out_shape=(...]
where the time goes in v4:
time: 79.4 us; the launch traced here: 79.2 us
  Pallas kernels  78.6 us (99%)
    pallas_call x1, Pallas kernels, shards(): pl.pallas_call(functools.partial(layer_kernel, planes, fsdp), out_shape=(...  75.4 us
    pallas_call x1, Pallas kernels, hand_over(): pl.pallas_call(hand_over_kernel, out_shape=(jax.ShapeDtypeStruct(dq.shape...  3.2 us

profile of v4, /device:TPU:0, one launch (start us, length us, event | category | flops | bytes accessed | tf_op | source)
XLA Modules:
  0.0 79.2 jit_solution(11897582065729038327)
XLA Ops:
  0.6 75.4 %layer.1 = (bf16[128,2048]{1,0:T(8,128)(2,1)}, bf16[2,128,2048]{2,1,0:T(8,128)(2,1)}, f32[64,2048]{1,0:T(8,128)}) custom-call(bf16[128,2048]{1,0:T(8,128)(2,1)} %bitcast.6, bf16[128,2,2048]{2,1,0:T(2,128)(2,1)} %bitcast.5, bf16[128,2048]{1,0:T(8,128)(2,1)} %bitcast.7, bf16[1024,2048]{1,0:T(8,128)(2,1)} %weight.1), custom_call_target="tpu_custom_call" | custom-call | tf_op jit(solution)/shard_map/layer/pallas_call | solution.py:600
  76.0 3.2 %hand_over.1 = (bf16[128,2048]{1,0:T(8,128)(2,1)}, bf16[128,2,2048]{2,1,0:T(2,128)(2,1)}, f32[64,2048]{1,0:T(8,128)}) custom-call(bf16[128,2048]{1,0:T(8,128)(2,1)} %get-tuple-element.9.dq_in, bf16[2,128,2048]{2,1,0:T(8,128)(2,1)} %get-tuple-element.10.kv_in, f32[64,2048]{1,0:T(8,128)} %get-tuple-element.11.w_in), custom_call_target="tpu_custom_call" | custom-call | tf_op jit(solution)/shard_map/hand_over/pallas_call | solution.py:572

commit v5 on v4

--- a/solution.py
+++ b/solution.py
@@ -28,7 +28,7 @@
     dq_out, kv_out, out_w,
     kv_raw, kv_in, q, kv, up, up_t, w, ga, att, low, bias, dq, dkv, dsum, q_next, ga_next, stats, stats_next,
     gw_out, gw_in, zw_out, pin, tin, fin_out, fin_in,
-    own_sem, kv_s, kv_r, q_s, q_r, u_s, u_r, w_s, w_r, kz_s, kz_r,
+    own_sem, kv_s, kv_r, q_s, q_r, u_s, u_r, w_s, w_r, wz_s, wz_r, kz_s, kz_r,
     dq_s, dq_r, dk_s, dk_r, qz_s, qz_r, gz_s, gz_r, st_s, st_r, gx_s, gx_r, pin_s, pin_r, tin_s, tin_r, f_s, f_r,
 ):
     toks = q_in.shape[0]
@@ -137,6 +137,21 @@
         here = w.at[w_rows(side(df)), head(c)]
         remote(here, here, w_s.at[df, c], w_r.at[df, c], dev(p, r, side(df))).wait_recv()
 
+    lower = lax.rem(p, 2) == 0
+    upper = jnp.logical_not(lower)
+    partner = dev(p + 1 - 2 * lax.rem(p, 2), r, f)
+
+    def wz_copy(df, c):
+        here = w.at[w_rows(side(df)), head(c)]
+        return remote(here, here, wz_s.at[df, c], wz_r.at[df, c], partner)
+
+    def by_side(c):
+        if c == heads - 2:
+            return lower
+        if c == heads - 1:
+            return upper
+        return None
+
     def kz_copy(d, c):
         src = kv_in.at[:, :, wide_head(r, c)] if d == 0 else kv.at[:, own_plane(peer[d]), head(c)]
         return remote(src, kv.at[:, rows(peer[d]), head(c)], kz_s.at[d, c], kz_r.at[d, c], dev(p + 1, r, f))
@@ -183,25 +198,24 @@
         def _():
             other()
 
-    def gx_copy(df, c):
+    def gx_copy(df, n, c):
         return remote(
-            gw_out.at[side(df), :, head(c)], gw_in.at[fsdp - df, :, head(c)], gx_s.at[df, c], gx_r.at[fsdp - df, c],
+            gw_out.at[side(df), n, :, head(c)], gw_in.at[fsdp - df, n, :, head(c)], gx_s.at[df, n, c], gx_r.at[fsdp - df, n, c],
             dev(p, r, side(df)),
         )
 
-    def gx_came(df, c):
-        here = gw_in.at[df, :, head(c)]
-        remote(here, here, gx_s.at[df, c], gx_r.at[df, c], dev(p, r, side(df))).wait_recv()
-
-    lower = lax.rem(p, 2) == 0
-    partner = dev(p + 1 - 2 * lax.rem(p, 2), r, f)
+    def gx_came(df, n, c):
+        here = gw_in.at[df, n, :, head(c)]
+        remote(here, here, gx_s.at[df, n, c], gx_r.at[df, n, c], dev(p, r, side(df))).wait_recv()
+
     group = lax.div(p, 2)
+    far_first = [lax.rem(2 * (group + 1) + i, planes) for i in range(planes - 2)] + [p + 1 - 2 * lax.rem(p, 2), p]
 
     def to_partner(n):
-        return jnp.logical_or(jnp.logical_and(lower, n > p), jnp.logical_and(jnp.logical_not(lower), n < p))
+        return jnp.logical_or(jnp.logical_and(lower, n > p), jnp.logical_and(upper, n < p))
 
     def to_plane(n):
-        return jnp.logical_or(jnp.logical_and(lower, n < p), jnp.logical_and(jnp.logical_not(lower), n > p))
+        return jnp.logical_or(jnp.logical_and(lower, n < p), jnp.logical_and(upper, n > p))
 
     def pin_copy(n, c):
         return remote(zw_out.at[n, :, head(c)], pin.at[n, :, head(c)], pin_s.at[n, c], pin_r.at[n, c], partner)
@@ -238,8 +252,22 @@
             kz_copy(0, c).start()
 
     def columns(c):
-        for df in range(1, fsdp):
-            w_copy(df, c).start()
+        def go():
+            for df in range(1, fsdp):
+                w_copy(df, c).start()
+
+        if by_side(c) is None:
+            go()
+        else:
+            pl.when(by_side(c))(go)
+
+    def pass_columns():
+        for c in (heads - 2, heads - 1):
+            @pl.when(by_side(c))
+            def _(c=c):
+                for df in range(1, fsdp):
+                    w_came(df, c)
+                    wz_copy(df, c).start()
 
     def lift():
         for h in range(2):
@@ -247,19 +275,19 @@
         for h in range(2):
             up_copy(1, h).start()
 
+    columns(2)
+    spread(0)
+    lift()
+    halo(0)
+    halo(1)
+    columns(0)
+    columns(3)
     columns(1)
+    halo(3)
+    spread(1)
+    spread(2)
+    spread(3)
     halo(2)
-    spread(2)
-    halo(0)
-    lift()
-    spread(0)
-    columns(3)
-    columns(2)
-    spread(3)
-    halo(3)
-    columns(0)
-    halo(1)
-    spread(1)
     row = lax.broadcasted_iota(jnp.int32, (toks, keys), 0)
     col = lax.broadcasted_iota(jnp.int32, (toks, keys), 1)
     for b in range(SPAN):
@@ -373,36 +401,35 @@
     def project(c, d):
         if d == 0:
             for df in range(1, fsdp):
-                w_came(df, c)
+                if by_side(c) is None:
+                    w_came(df, c)
+                else:
+                    pl.when(jnp.logical_not(by_side(c)))(lambda df=df: wz_copy(df, c).wait_recv())
         ga[rows(peer[d]), head(c)] = jnp.dot(up[rows(peer[d]), :], w[:, head(c)], preferred_element_type=F32).astype(BF16)
 
     def turn(d):
         up_t[:, rows(peer[d])] = up[rows(peer[d]), :].T
 
-    tile = plane_toks
-    unit = fsdp * own_rows
+    tile = up_in.shape[1] // planes
 
     def weigh(c):
-        def step(t, _):
-            value = jnp.dot(up_t[pl.ds(pl.multiple_of(t * tile, tile), tile), :], att[:, head(c)], preferred_element_type=F32)
-            value = value.reshape(tile // unit, fsdp, own_rows, HEAD_DIM)
-            part = tile // fsdp
-            for n in range(fsdp):
-                gw_out[n, pl.ds(pl.multiple_of(t * part, part), part), head(c)] = value[:, n].reshape(part, HEAD_DIM).astype(BF16)
-            return 0
-
-        lax.fori_loop(0, up_t.shape[0] // tile, step, 0)
-        for df in range(1, fsdp):
-            gx_copy(df, c).start()
+        for n in far_first:
+            rows_n = pl.ds(pl.multiple_of(n * tile, tile), tile)
+            value = jnp.dot(up_t[rows_n, :], att[:, head(c)], preferred_element_type=F32)
+            value = value.reshape(SPAN, fsdp, own_rows, HEAD_DIM)
+            for i in range(fsdp):
+                gw_out[i, n, :, head(c)] = value[:, i].reshape(plane_rows, HEAD_DIM).astype(BF16)
+            for df in range(1, fsdp):
+                gx_copy(df, n, c).start()
 
     def merge(c):
-        total = gw_out[f, :, head(c)].astype(F32)
-        for df in range(1, fsdp):
-            gx_came(df, c)
-            total = total + gw_in[df, :, head(c)].astype(F32)
-        for n in range(planes):
-            zw_out[n, :, head(c)] = total[n * plane_rows : (n + 1) * plane_rows].astype(BF16)
-        for n in range(planes):
+        for n in far_first:
+            total = gw_out[f, n, :, head(c)].astype(F32)
+            for df in range(1, fsdp):
+                gx_came(df, n, c)
+                total = total + gw_in[df, n, :, head(c)].astype(F32)
+            zw_out[n, :, head(c)] = total.astype(BF16)
+
             @pl.when(to_partner(n))
             def _(n=n):
                 pin_copy(n, c).start()
@@ -461,66 +488,67 @@
         project(c, 2)
         project(c, 3)
 
+    forward_q(0)
+    forward(0)
+    pass_columns()
+    lift_on(0)
     settle()
-    lift_on(0)
+    attend(0)
+    lift_on(1)
+    project_chip(1)
+    project_chip(0)
+    lift_end()
+    project_rest(0)
+    forward(1)
+    send_down(0)
+    backward(0)
+    weigh(0)
+    project_chip(2)
+    forward_q(1)
     forward(2)
-    lift_on(1)
+    project_rest(2)
+    project_rest(1)
     forward_q(2)
+    attend(1)
+    send_down(1)
+    weigh(1)
+    merge(0)
     attend(2)
-    project_chip(2)
-    lift_end()
-    project_rest(2)
-    forward(0)
+    project_chip(3)
+    forward(3)
+    weigh(2)
+    merge(1)
+    relay(0)
+    next_plane(0)
     send_down(2)
-    weigh(2)
-    forward_q(0)
-    forward(3)
-    project_chip(0)
-    project_rest(0)
+    return_kv(0)
     forward_q(3)
-    attend(0)
-    send_down(0)
-    project_chip(1)
-    project_chip(3)
+    attend(3)
     project_rest(3)
-    forward(1)
-    weigh(0)
-    forward_q(1)
-    attend(3)
-    merge(2)
+    relay(1)
     weigh(3)
     send_down(3)
-    attend(1)
+    backward(2)
+    backward(1)
+    backward(3)
+    merge(2)
+    next_plane(1)
+    return_kv(1)
     next_plane(2)
-    project_rest(1)
-    merge(0)
-    backward(2)
-    send_down(1)
+    total_up(0)
+    total_up(1)
+    relay(2)
+    merge(3)
+    next_plane(3)
     return_kv(2)
-    backward(0)
-    weigh(1)
-    next_plane(0)
-    return_kv(0)
-    relay(2)
-    backward(3)
-    merge(3)
-    relay(0)
-    next_plane(3)
+    relay(3)
     return_kv(3)
-    next_plane(1)
-    merge(1)
-    relay(3)
-    total_up(0)
-    backward(1)
+    total_up(2)
+    finish(1)
+    total_up(3)
+    finish(2)
     finish(0)
-    return_kv(1)
-    total_up(2)
-    relay(1)
-    total_up(3)
-    total_up(1)
     finish(3)
-    finish(2)
-    finish(1)
     for c in range(heads):
         for d in around:
             dq_came(d, c)
@@ -531,8 +559,16 @@
             hand(j, lambda: own_dq(j, c).wait(), lambda: dq_copy(j, c).wait_send())
             hand(j, lambda: own_dk(j, c).wait(), lambda: dk_copy(j, c).wait_send())
         for df in range(1, fsdp):
-            w_copy(df, c).wait_send()
-            gx_copy(df, c).wait_send()
+            if by_side(c) is None:
+                w_copy(df, c).wait_send()
+            else:
+                @pl.when(by_side(c))
+                def _(c=c, df=df):
+                    w_copy(df, c).wait_send()
+                    wz_copy(df, c).wait_send()
+
+            for n in range(planes):
+                gx_copy(df, n, c).wait_send()
         for n in range(planes):
             @pl.when(to_partner(n))
             def _(n=n, c=c):
@@ -597,6 +633,7 @@
     near = dma((SPAN, heads))
     sides = dma((fsdp, heads))
     levels = dma((planes, heads))
+    parts = dma((fsdp, planes, heads))
     dq, out_kv, out_w = pl.pallas_call(
         functools.partial(layer_kernel, planes, fsdp),
         out_shape=(
@@ -625,15 +662,15 @@
             pltpu.VMEM((group, quarter), BF16),
             pltpu.VMEM((heads, 8, group), F32),
             pltpu.VMEM((heads, 8, group), F32),
-            pltpu.VMEM((fsdp, model // fsdp, quarter), BF16),
-            pltpu.VMEM((fsdp, model // fsdp, quarter), BF16),
+            pltpu.VMEM((fsdp, planes, SPAN * own_rows, quarter), BF16),
+            pltpu.VMEM((fsdp, planes, SPAN * own_rows, quarter), BF16),
             pltpu.VMEM((planes, SPAN * own_rows, quarter), BF16),
             pltpu.VMEM((planes, SPAN * own_rows, quarter), BF16),
             pltpu.VMEM((planes // 2, SPAN * own_rows, quarter), BF16),
             pltpu.VMEM((SPAN, own_rows, quarter), BF16),
             pltpu.VMEM((SPAN, own_rows, quarter), BF16),
-            dma((4,)), near, near, near, near, dma((SPAN, 2)), dma((SPAN, 2)), sides, sides, near, near,
-            near, near, near, near, near, near, dma((heads,)), dma((heads,)), dma((heads,)), dma((heads,)), sides, sides, levels, levels, levels, dma((planes // 2, heads)), near, near,
+            dma((4,)), near, near, near, near, dma((SPAN, 2)), dma((SPAN, 2)), sides, sides, sides, sides, near, near,
+            near, near, near, near, near, near, dma((heads,)), dma((heads,)), dma((heads,)), dma((heads,)), parts, parts, levels, levels, levels, dma((planes // 2, heads)), near, near,
         ],
         compiler_params=pltpu.CompilerParams(collective_id=0, has_side_effects=True),
         name="layer",

time: 79.4 us -> 78.1 us (0.984)
  Pallas kernels: 78.6 us -> 77.3 us
    pallas_call x1, Pallas kernels: 75.4 us -> 74.1 us  [shards(): pl.pallas_call(functools.partial(layer_kernel, planes, fsdp), out_shape=(...]
where the time goes in v5:
time: 78.1 us; the launch traced here: 77.9 us
  Pallas kernels  77.3 us (99%)
    pallas_call x1, Pallas kernels, shards(): pl.pallas_call(functools.partial(layer_kernel, planes, fsdp), out_shape=(...  74.1 us
    pallas_call x1, Pallas kernels, hand_over(): pl.pallas_call(hand_over_kernel, out_shape=(jax.ShapeDtypeStruct(dq.shape...  3.2 us

profile of v5, /device:TPU:0, one launch (start us, length us, event | category | flops | bytes accessed | tf_op | source)
XLA Modules:
  0.0 77.9 jit_solution(11984475799579934731)
XLA Ops:
  0.6 74.1 %layer.1 = (bf16[128,2048]{1,0:T(8,128)(2,1)}, bf16[2,128,2048]{2,1,0:T(8,128)(2,1)}, f32[64,2048]{1,0:T(8,128)}) custom-call(bf16[128,2048]{1,0:T(8,128)(2,1)} %bitcast.6, bf16[128,2,2048]{2,1,0:T(2,128)(2,1)} %bitcast.5, bf16[128,2048]{1,0:T(8,128)(2,1)} %bitcast.7, bf16[1024,2048]{1,0:T(8,128)(2,1)} %weight.1), custom_call_target="tpu_custom_call" | custom-call | tf_op jit(solution)/shard_map/layer/pallas_call | solution.py:637
  74.7 3.2 %hand_over.1 = (bf16[128,2048]{1,0:T(8,128)(2,1)}, bf16[128,2,2048]{2,1,0:T(2,128)(2,1)}, f32[64,2048]{1,0:T(8,128)}) custom-call(bf16[128,2048]{1,0:T(8,128)(2,1)} %get-tuple-element.9.dq_in, bf16[2,128,2048]{2,1,0:T(8,128)(2,1)} %get-tuple-element.10.kv_in, f32[64,2048]{1,0:T(8,128)} %get-tuple-element.11.w_in), custom_call_target="tpu_custom_call" | custom-call | tf_op jit(solution)/shard_map/hand_over/pallas_call | solution.py:608

commit v6 on v5

--- a/solution.py
+++ b/solution.py
@@ -236,9 +236,11 @@
 
     around = range(1, SPAN)
 
-    def spread(c):
+    def spread_kv(c):
         for d in around:
             kv_copy(d, c).start()
+
+    def spread_q(c):
         for d in around:
             q_copy(d, c).start()
 
@@ -275,19 +277,23 @@
         for h in range(2):
             up_copy(1, h).start()
 
-    columns(2)
-    spread(0)
-    lift()
     halo(0)
     halo(1)
+    spread_kv(0)
+    spread_q(0)
     columns(0)
+    columns(2)
+    spread_q(1)
     columns(3)
+    lift()
+    spread_q(2)
+    spread_kv(1)
+    halo(2)
+    spread_q(3)
+    halo(3)
+    spread_kv(2)
     columns(1)
-    halo(3)
-    spread(1)
-    spread(2)
-    spread(3)
-    halo(2)
+    spread_kv(3)
     row = lax.broadcasted_iota(jnp.int32, (toks, keys), 0)
     col = lax.broadcasted_iota(jnp.int32, (toks, keys), 1)
     for b in range(SPAN):
@@ -488,66 +494,66 @@
         project(c, 2)
         project(c, 3)
 
+    forward(0)
+    settle()
+    forward_q(1)
+    project_chip(0)
     forward_q(0)
-    forward(0)
     pass_columns()
+    attend(0)
     lift_on(0)
-    settle()
-    attend(0)
     lift_on(1)
-    project_chip(1)
-    project_chip(0)
+    forward_q(2)
     lift_end()
     project_rest(0)
-    forward(1)
-    send_down(0)
-    backward(0)
     weigh(0)
     project_chip(2)
-    forward_q(1)
+    send_down(0)
+    project_chip(1)
+    forward(1)
+    project_chip(3)
+    project_rest(2)
+    backward(0)
+    forward_q(3)
     forward(2)
-    project_rest(2)
     project_rest(1)
-    forward_q(2)
+    merge(0)
     attend(1)
     send_down(1)
     weigh(1)
-    merge(0)
+    backward(1)
+    forward(3)
     attend(2)
-    project_chip(3)
-    forward(3)
+    send_down(2)
     weigh(2)
-    merge(1)
     relay(0)
     next_plane(0)
-    send_down(2)
-    return_kv(0)
-    forward_q(3)
+    merge(1)
+    backward(2)
+    next_plane(2)
     attend(3)
+    total_up(0)
+    merge(2)
     project_rest(3)
+    return_kv(2)
     relay(1)
     weigh(3)
+    finish(0)
+    return_kv(0)
     send_down(3)
-    backward(2)
-    backward(1)
-    backward(3)
-    merge(2)
+    total_up(1)
     next_plane(1)
     return_kv(1)
-    next_plane(2)
-    total_up(0)
-    total_up(1)
     relay(2)
     merge(3)
+    backward(3)
     next_plane(3)
-    return_kv(2)
     relay(3)
     return_kv(3)
     total_up(2)
     finish(1)
     total_up(3)
     finish(2)
-    finish(0)
     finish(3)
     for c in range(heads):
         for d in around:
@@ -604,16 +610,20 @@
 
 def hand_over(dq, kv, w):
     toks, width = dq.shape
-    vm = pl.BlockSpec(memory_space=pltpu.VMEM)
+    steps = 2
+    part = toks // steps
+    whole = pl.BlockSpec(w.shape, lambda i: (0, 0))
+    piece = pl.BlockSpec((part, width), lambda i: (i, 0))
     return pl.pallas_call(
         hand_over_kernel,
+        grid=(steps,),
         out_shape=(
             jax.ShapeDtypeStruct(dq.shape, dq.dtype),
             jax.ShapeDtypeStruct((toks, 2, width), kv.dtype),
             jax.ShapeDtypeStruct(w.shape, w.dtype),
         ),
-        in_specs=[vm] * 3,
-        out_specs=(vm,) * 3,
+        in_specs=[piece, pl.BlockSpec((2, part, width), lambda i: (0, i, 0)), whole],
+        out_specs=(piece, pl.BlockSpec((part, 2, width), lambda i: (i, 0, 0)), whole),
         name="hand_over",
     )(dq, kv, w)
 

time: 78.1 us -> 77.4 us (level)
  no operation moved by 1% of the time
where the time goes in v6:
time: 77.4 us; the launch traced here: 77.2 us
  Pallas kernels  76.6 us (99%)
    pallas_call x1, Pallas kernels, shards(): pl.pallas_call(functools.partial(layer_kernel, planes, fsdp), out_shape=(...  73.8 us
    pallas_call x1, Pallas kernels, hand_over(): pl.pallas_call(hand_over_kernel, grid=(steps,), out_shape=(jax.ShapeDtype...  2.79 us

profile of v6, /device:TPU:0, one launch (start us, length us, event | category | flops | bytes accessed | tf_op | source)
XLA Modules:
  0.0 77.2 jit_solution(16015684000690810631)
XLA Ops:
  0.6 73.8 %layer.1 = (bf16[128,2048]{1,0:T(8,128)(2,1)}, bf16[2,128,2048]{2,1,0:T(8,128)(2,1)}, f32[64,2048]{1,0:T(8,128)}) custom-call(bf16[128,2048]{1,0:T(8,128)(2,1)} %bitcast.6, bf16[128,2,2048]{2,1,0:T(2,128)(2,1)} %bitcast.5, bf16[128,2048]{1,0:T(8,128)(2,1)} %bitcast.7, bf16[1024,2048]{1,0:T(8,128)(2,1)} %weight.1), custom_call_target="tpu_custom_call" | custom-call | tf_op jit(solution)/shard_map/layer/pallas_call | solution.py:647
  74.4 2.8 %hand_over.1 = (bf16[128,2048]{1,0:T(8,128)(2,1)}, bf16[128,2,2048]{2,1,0:T(2,128)(2,1)}, f32[64,2048]{1,0:T(8,128)}) custom-call(bf16[128,2048]{1,0:T(8,128)(2,1)} %get-tuple-element.9.dq_in, bf16[2,128,2048]{2,1,0:T(8,128)(2,1)} %get-tuple-element.10.kv_in, f32[64,2048]{1,0:T(8,128)} %get-tuple-element.11.w_in), custom_call_target="tpu_custom_call" | custom-call | tf_op jit(solution)/shard_map/hand_over/pallas_call | solution.py:617

commit v7 on v6

--- a/solution.py
+++ b/solution.py
@@ -466,6 +466,34 @@
         out_w[:, wide_head(r, c)] = fin_out[r, :, head(c)].astype(F32)
         for d in around:
             out_w[:, wide_head(peer[d], c)] = fin_in[peer[d], :, head(c)].astype(F32)
+
+    def drain():
+        for c in range(heads):
+            for d in around:
+                kv_copy(d, c).wait_send()
+                q_copy(d, c).wait_send()
+            for df in range(1, fsdp):
+                if by_side(c) is None:
+                    w_copy(df, c).wait_send()
+                else:
+                    @pl.when(by_side(c))
+                    def _(c=c, df=df):
+                        w_copy(df, c).wait_send()
+                        wz_copy(df, c).wait_send()
+
+            @pl.when(not_last)
+            def _(c=c):
+                for d in range(SPAN):
+                    kz_copy(d, c).wait_send()
+
+            @pl.when(not_first)
+            def _(c=c):
+                for d in range(SPAN):
+                    qz_copy(d, c).wait_send()
+
+        for d in around:
+            for h in range(2):
+                up_copy(d, h).wait_send()
 
     def settle():
         kv[:, own_plane(r), :] = kv_in[:, :, quart(r)]
@@ -552,6 +580,7 @@
     return_kv(3)
     total_up(2)
     finish(1)
+    drain()
     total_up(3)
     finish(2)
     finish(3)
@@ -559,20 +588,11 @@
         for d in around:
             dq_came(d, c)
             dk_came(d, c)
-            for copy in (kv_copy(d, c), q_copy(d, c), f_copy(d, c)):
-                copy.wait_send()
+            f_copy(d, c).wait_send()
         for j in range(SPAN):
             hand(j, lambda: own_dq(j, c).wait(), lambda: dq_copy(j, c).wait_send())
             hand(j, lambda: own_dk(j, c).wait(), lambda: dk_copy(j, c).wait_send())
         for df in range(1, fsdp):
-            if by_side(c) is None:
-                w_copy(df, c).wait_send()
-            else:
-                @pl.when(by_side(c))
-                def _(c=c, df=df):
-                    w_copy(df, c).wait_send()
-                    wz_copy(df, c).wait_send()
-
             for n in range(planes):
                 gx_copy(df, n, c).wait_send()
         for n in range(planes):
@@ -584,21 +604,10 @@
             def _(n=n, c=c):
                 tin_copy(n, c).wait_send()
 
-        @pl.when(not_last)
-        def _(c=c):
-            for d in range(SPAN):
-                kz_copy(d, c).wait_send()
-
         @pl.when(not_first)
         def _(c=c):
-            for d in range(SPAN):
-                qz_copy(d, c).wait_send()
             ga_copy(c).wait_send()
             stats_copy(c).wait_send()
-
-    for d in around:
-        for h in range(2):
-            up_copy(d, h).wait_send()
 
 
 def hand_over_kernel(dq_in, kv_in, w_in, dq_out, kv_out, w_out):

time: 77.4 us -> 77.3 us (level)
  no operation moved by 1% of the time
where the time goes in v7:
time: 77.3 us; the launch traced here: 77.1 us
  Pallas kernels  76.5 us (99%)
    pallas_call x1, Pallas kernels, shards(): pl.pallas_call(functools.partial(layer_kernel, planes, fsdp), out_shape=(...  73.7 us
    pallas_call x1, Pallas kernels, hand_over(): pl.pallas_call(hand_over_kernel, grid=(steps,), out_shape=(jax.ShapeDtype...  2.79 us

profile of v7, /device:TPU:0, one launch (start us, length us, event | category | flops | bytes accessed | tf_op | source)
XLA Modules:
  0.0 77.1 jit_solution(13720021516815012291)
XLA Ops:
  0.6 73.7 %layer.1 = (bf16[128,2048]{1,0:T(8,128)(2,1)}, bf16[2,128,2048]{2,1,0:T(8,128)(2,1)}, f32[64,2048]{1,0:T(8,128)}) custom-call(bf16[128,2048]{1,0:T(8,128)(2,1)} %bitcast.6, bf16[128,2,2048]{2,1,0:T(2,128)(2,1)} %bitcast.5, bf16[128,2048]{1,0:T(8,128)(2,1)} %bitcast.7, bf16[1024,2048]{1,0:T(8,128)(2,1)} %weight.1), custom_call_target="tpu_custom_call" | custom-call | tf_op jit(solution)/shard_map/layer/pallas_call | solution.py:656
  74.3 2.8 %hand_over.1 = (bf16[128,2048]{1,0:T(8,128)(2,1)}, bf16[128,2,2048]{2,1,0:T(2,128)(2,1)}, f32[64,2048]{1,0:T(8,128)}) custom-call(bf16[128,2048]{1,0:T(8,128)(2,1)} %get-tuple-element.9.dq_in, bf16[2,128,2048]{2,1,0:T(8,128)(2,1)} %get-tuple-element.10.kv_in, f32[64,2048]{1,0:T(8,128)} %get-tuple-element.11.w_in), custom_call_target="tpu_custom_call" | custom-call | tf_op jit(solution)/shard_map/hand_over/pallas_call | solution.py:626
